TPU v7x, 256 devices: a whole 4x4x8 slice. The times are simulated.
256 devices in a mesh: dp: 32 (over x, z), section: 8 (over y, core).
Axes of the slice: x: 4, y: 4, z: 8, core: 2. Of those that a mesh axis runs over, the one named last changes fastest.
Arguments:
- tap_maps: bfloat16 [4, 2, 4096, 3200], P(None, None, ('dp', 'section')), may hold values from -6 to 6
- lateral_weight: bfloat16 [8, 3200, 768], P('section', 'dp'), may hold values from -0.109375 to 0.109375
- conv_weight: bfloat16 [8, 6912, 768], P('section'), may hold values from -0.078125 to 0.078125
- classifier: bfloat16 [768, 150], replicated, may hold values from -0.875 to 0.875
- tile_counts: int32 [32, 2], P('dp'), may hold values from 1 to 2, as said below
- labels: int32 [2, 4096], P(None, 'dp'), may hold values from 0 to 149
Outputs:
- conv_grad: float32 [8, 6912, 768], P('section', 'dp')
- lateral_grad: float32 [8, 3200, 768], P('section', 'dp')
Inputs may be any that keep to these rules, and one draw needn't show every extreme that they name: `tile_counts`: some entry equals 2.
All inputs are finite; a program needn't handle non-finite values.
Results may differ from a plain program's by a relative error of at most 0.035.
Values may be sent and summed in bfloat16 or wider, within the bound.
A program may use at most 128 MiB of HBM per device.

v0:
```python
import jax
import jax.numpy as jnp
from jax import lax
from jax.sharding import PartitionSpec as P

TILE_CAP = 2
BAND_ROWS = 1
BAND_COLS = 64


def padded_2(shard, sides, width):
    for axis, dim in sides:
        size, length = (lax.axis_size(axis), shard.shape[dim])
        up = [(i, (i + 1) % size) for i in range(size - 1)]
        down = [(j, i) for i, j in up]
        last = lax.slice_in_dim(shard, length - width, length, axis=dim)
        initial = lax.slice_in_dim(shard, 0, width, axis=dim)
        before = lax.ppermute(last, axis, up)
        after = lax.ppermute(initial, axis, down)
        shard = jnp.concatenate([before, shard, after], axis=dim)
    return shard


def shifted(block, axis, distance):
    devices = range(lax.axis_size(axis))
    route = [(i - distance, i) for i in devices if i - distance in devices]
    return lax.ppermute(block, axis, route)


def neighbour_shifts():
    return [(row_shift, col_shift) for row_shift in (-1, 0, 1) for col_shift in (-1, 0, 1)]


def widen(summed):
    grid = summed.reshape(TILE_CAP, BAND_ROWS, BAND_COLS, summed.shape[-1])
    return padded_2(grid, (("dp", 1),), 1)


def gather_columns(widened):
    chans = widened.shape[-1]
    padded = jnp.pad(widened, ((0, 0), (0, 0), (1, 1), (0, 0)))
    pieces = [
        padded[:, 1 + rs : 1 + rs + BAND_ROWS, 1 + cs : 1 + cs + BAND_COLS, :]
        for rs, cs in neighbour_shifts()
    ]
    return jnp.concatenate(pieces, axis=-1).reshape(-1, 9 * chans)


def spread_columns(grad_cols):
    chans = grad_cols.shape[-1] // 9
    grid = grad_cols.reshape(TILE_CAP, BAND_ROWS, BAND_COLS, 9, chans)
    total = jnp.zeros((TILE_CAP, BAND_ROWS + 2, BAND_COLS + 2, chans), jnp.float32)
    for offset, (rs, cs) in enumerate(neighbour_shifts()):
        total = total + jnp.pad(
            grid[:, :, :, offset, :], ((0, 0), (1 + rs, 1 - rs), (1 + cs, 1 - cs), (0, 0))
        )
    inner = total[:, 1:-1, 1:-1, :]
    rims = jnp.stack([total[:, 0, 1:-1, :], total[:, BAND_ROWS + 1, 1:-1, :]], axis=1)
    return (inner, rims)


def on_device(tap_maps, lateral_weight, conv_weight, classifier, tile_counts, labels):
    sections = lax.axis_size("section")
    groups = lax.axis_size("dp")
    place = lax.axis_index("section")
    levels = tap_maps.shape[0]
    micros = tap_maps.shape[1]
    width = tap_maps.shape[3]
    pixels = labels.shape[1]
    chans = conv_weight.shape[2]
    classes = classifier.shape[1]
    gathered = lax.all_gather(tap_maps, "section", axis=2, tiled=True)
    routed = lax.dynamic_index_in_dim(gathered, place * levels // sections, 0, keepdims=False)
    tap_rows = routed.reshape(micros * pixels, width)
    left = tap_rows
    lateral = jnp.dot(
        left,
        lax.all_gather(lateral_weight[0], "dp", axis=0, tiled=True),
        preferred_element_type=jnp.float32,
    )
    lateral = lateral.reshape(micros, pixels, chans)
    weights = conv_weight[0]
    ticks = sections + micros - 1

    def forward(step_count, carry):
        outgoing, widened_store, preact_store = carry
        incoming = shifted(outgoing, "section", 1)
        micro = step_count - place
        active = jnp.logical_and(micro >= 0, micro < micros)
        which = jnp.clip(micro, 0, micros - 1)
        summed = (
            incoming.astype(jnp.float32)
            + lax.dynamic_index_in_dim(lateral, which, 0, keepdims=False)
        ).astype(jnp.bfloat16)
        widened = widen(summed)

        def forward_advance(operands):
            extended, widened_old, preact_old = operands
            preact = jnp.dot(gather_columns(extended), weights, preferred_element_type=jnp.float32)
            activated = jax.nn.silu(preact).astype(jnp.bfloat16)
            return (
                activated,
                lax.dynamic_update_index_in_dim(widened_old, extended, which, 0),
                lax.dynamic_update_index_in_dim(preact_old, preact, which, 0),
            )

        def forward_skipped(operands):
            return (jnp.zeros((pixels, chans), jnp.bfloat16), operands[1], operands[2])

        return lax.cond(
            active, forward_advance, forward_skipped, (widened, widened_store, preact_store)
        )

    start_state = (
        jnp.zeros((pixels, chans), jnp.bfloat16),
        jnp.zeros((micros, TILE_CAP, BAND_ROWS + 2, BAND_COLS, chans), jnp.bfloat16),
        jnp.zeros((micros, pixels, chans), jnp.float32),
    )
    _, widened_store, preact_store = lax.fori_loop(0, ticks, forward, start_state)
    band = BAND_ROWS * BAND_COLS
    slot_ids = jnp.arange(pixels) // band
    per_count = tile_counts[0][:, None]
    valid = (slot_ids[None, :] < per_count).astype(jnp.float32)
    pixel_weight = valid / (per_count.astype(jnp.float32) * band * groups * micros)
    is_last = place == sections - 1
    class_ids = jnp.arange(classes)

    def backward(step_count, carry):
        outgoing, grad_pre_store, grad_in_store = carry
        incoming = shifted(outgoing, "section", -1)
        micro = step_count - (sections - 1 - place)
        active = jnp.logical_and(micro >= 0, micro < micros)
        which = jnp.clip(micro, 0, micros - 1)

        def backward_advance(operands):
            arrived, grad_pre_old = operands
            preact = lax.dynamic_index_in_dim(preact_store, which, 0, keepdims=False)
            activated = jax.nn.silu(preact).astype(jnp.bfloat16)
            logits = jnp.dot(activated, classifier, preferred_element_type=jnp.float32)
            expo = jnp.exp(logits)
            probs = expo / jnp.sum(expo, axis=-1, keepdims=True)
            label_row = lax.dynamic_index_in_dim(labels, which, 0, keepdims=False)
            onehot = (label_row[:, None] == class_ids[None, :]).astype(jnp.float32)
            weight_row = lax.dynamic_index_in_dim(pixel_weight, which, 0, keepdims=False)
            grad_logits = ((probs - onehot) * weight_row[:, None]).astype(jnp.bfloat16)
            from_loss = lax.dot_general(
                grad_logits,
                classifier,
                (((1,), (1,)), ((), ())),
                preferred_element_type=jnp.float32,
            )
            grad_out = jnp.where(is_last, from_loss, arrived.astype(jnp.float32))
            sigma = jax.nn.sigmoid(preact)
            grad_pre = (grad_out * sigma * (1.0 + preact * (1.0 - sigma))).astype(jnp.bfloat16)
            grad_cols = lax.dot_general(
                grad_pre, weights, (((1,), (1,)), ((), ())), preferred_element_type=jnp.float32
            )
            inner, rims = spread_columns(grad_cols)
            return (inner, rims, lax.dynamic_update_index_in_dim(grad_pre_old, grad_pre, which, 0))

        def backward_skipped(operands):
            return (
                jnp.zeros((TILE_CAP, BAND_ROWS, BAND_COLS, chans), jnp.float32),
                jnp.zeros((TILE_CAP, 2, BAND_COLS, chans), jnp.float32),
                operands[1],
            )

        inner, rims, grad_pre_store = lax.cond(
            active, backward_advance, backward_skipped, (incoming, grad_pre_store)
        )
        received = padded_2(rims.astype(jnp.bfloat16), (("dp", 1),), 1).astype(rims.dtype)
        inner = inner.at[:, 0].add(received[:, 0])
        inner = inner.at[:, BAND_ROWS - 1].add(received[:, 3])
        grad_in = inner.reshape(pixels, chans).astype(jnp.bfloat16)
        updated = lax.dynamic_update_index_in_dim(grad_in_store, grad_in, which, 0)
        grad_in_store = jnp.where(active, updated, grad_in_store)
        return (grad_in, grad_pre_store, grad_in_store)

    back_state = (
        jnp.zeros((pixels, chans), jnp.bfloat16),
        jnp.zeros((micros, pixels, chans), jnp.bfloat16),
        jnp.zeros((micros, pixels, chans), jnp.bfloat16),
    )
    _, grad_pre_store, grad_in_store = lax.fori_loop(0, ticks, backward, back_state)
    grad_pre_rows = grad_pre_store.reshape(micros * pixels, chans)
    grad_in_rows = grad_in_store.reshape(micros * pixels, chans)
    column_rows = gather_columns(
        widened_store.reshape(micros * TILE_CAP, BAND_ROWS + 2, BAND_COLS, chans)
    )
    left = tap_rows
    lateral_grad = lax.psum_scatter(
        lax.dot_general(
            left, grad_in_rows, (((0,), (0,)), ((), ())), preferred_element_type=jnp.float32
        ).astype(jnp.bfloat16),
        "dp",
        scatter_dimension=0,
        tiled=True,
    ).astype(jnp.float32)
    left = column_rows
    conv_grad = lax.psum_scatter(
        lax.dot_general(
            left, grad_pre_rows, (((0,), (0,)), ((), ())), preferred_element_type=jnp.float32
        ).astype(jnp.bfloat16),
        "dp",
        scatter_dimension=0,
        tiled=True,
    ).astype(jnp.float32)
    return (conv_grad[None], lateral_grad[None])


def solution(mesh):
    placed = (
        P(None, None, ("dp", "section"), None),
        P("section", "dp", None),
        P("section", None, None),
        P(),
        P("dp", None),
        P(None, "dp"),
    )
    return jax.shard_map(
        on_device,
        mesh=mesh,
        in_specs=placed,
        out_specs=(P("section", "dp", None), P("section", "dp", None)),
        check_vma=False,
    )
```

profile of v0, /device:TPU:2, one launch (start us, length us, event | category | flops | bytes accessed | tf_op | source)
XLA Modules:
  0.0 1170.3 jit_solution(1554315526162453511)
XLA Ops:
  10.9 46.5 %all-gather.4.cloned.1.call-done = bf16[4,2,128,3200]{3,2,1,0:T(8,128)(2,1)} async-done(((bf16[4,2,16,3200]{3,2,1,0:T(8,128)(2,1)}), bf16[4,2,128,3200]{3,2,1,0:T(8,128)(2,1)}) %all-gather.4.cloned.1.call-update) | async-done | bytes 6553616 | tf_op jit(solution)/shard_map/all_gather | solution.py:72
  59.0 106.1 %all-gather.6.cloned.1.call-done = bf16[1,3200,768]{2,0,1:T(2,128)(2,1)} async-done(((bf16[1,100,768]{2,0,1:T(2,128)(2,1)}), bf16[1,3200,768]{2,0,1:T(2,128)(2,1)}) %all-gather.6.cloned.1.call-update) | async-done | bytes 4915216 | tf_op jit(solution)/shard_map/all_gather | solution.py:78
  172.2 189.4 %while.43 = (s32[]{:T(128)}, bf16[128,768]{1,0:T(8,128)(2,1)}, bf16[2,2,3,64,768]{4,3,2,1,0:T(8,128)(2,1)S(1)}, f32[2,128,768]{2,1,0:T(8,128)}, s32[]{:T(128)}, ...) while((s32[]{:T(128)}, bf16[128,768]{1,0:T(8,128)(2,1)}, ...), condition=%wide.region_3.4_spmd, body=%wide.region_0.3_spmd.sunk | while | flops 1360330752 | bytes 25166232 | solution.py:119
  186.0 7.6 conditional.5
  186.5 6.3 multiply_convert_fusion
  209.3 7.6 conditional.5
  209.7 6.3 multiply_convert_fusion
  234.4 9.5 collective-permute-start
  247.1 6.2 collective-permute-start.1
  265.3 6.2 collective-permute-start.1
  275.4 13.1 %collective-permute-start = (bf16[128,768]{1,0:T(8,128)(2,1)}, bf16[128,768]{1,0:T(8,128)(2,1)S(1)}, u32[]{:S(2)}, u32[]{:S(2)}) collective-permute-start(bf16[128,768]{1,0:T(8,128)(2,1)} %get-tuple-element.891), channel_id=1, source_target_pairs={{0,1},{1,2},{2,3},{3,4},{4,5},{5,6},{6,7},{8,9},{9,10},{10,11},{11... | collective-permute-start | bytes 589832 | tf_op jit(solution)/shard_map/while/body/eval_jaxpr/ppermute | solution.py:27
  291.8 6.2 collective-permute-start.1
  301.9 6.2 collective-permute-start
  321.5 7.1 collective-permute-start
  331.8 6.2 collective-permute-start.1
  342.0 6.2 collective-permute-start
  365.7 560.7 %while.44 = (s32[]{:T(128)}, bf16[128,768]{1,0:T(8,128)(2,1)S(1)}, bf16[2,128,768]{2,1,0:T(8,128)(2,1)}, bf16[2,128,768]{2,1,0:T(8,128)(2,1)}, s32[]{:T(128)}, /...) while((s32[]{:T(128)}, bf16[128,768]{1,0:T(8,128)(2,1)S(1)}, ...), condition=%wide.region_8.9_spmd.clone, body=%wide.region_4.8_spmd.clone.sunk | while | flops 1424437120 | bytes 46599908 | solution.py:184
  367.1 6.3 collective-permute-done.3
  388.7 6.5 collective-permute-done.5
  430.9 6.6 collective-permute-done.3
  490.7 6.3 collective-permute-done.3
  520.6 7.8 collective-permute-done.3
  581.1 226.5 %collective-permute-done.3 = bf16[128,768]{1,0:T(8,128)(2,1)S(1)} collective-permute-done((bf16[128,768]{1,0:T(8,128)(2,1)S(1)}, bf16[128,768]{1,0:T(8,128)(2,1)S(1)}, u32[]{:S(2)}, u32[]{:S(2)}) %collective-permute-start.3) | collective-permute-done | bytes 196640 | tf_op jit(solution)/shard_map/while/body/eval_jaxpr/ppermute | solution.py:27
  807.6 34.2 %conditional.6 = (f32[2,1,64,768]{3,1,2,0:T(1,128)}, bf16[2,2,64,768]{3,1,2,0:T(2,128)(2,1)}, bf16[2,128,768]{2,1,0:T(8,128)(2,1)}) conditional(s32[]{:T(128)} %convert_element_type.205, bf16[2,128,768]{2,1,0:T(8,128)(2,1)} %get-tuple-element.928, (pred[]{:T(512)}, s32[]{:T(128)}, f32[2,128,768]{2,1,0:T(8,128)}, bf16[768,150]{1,0:T(8,128)(2,1)}, ...), branch_computations={%region_5.5_spmd, %region_6.7_spmd} | conditional | flops 1422863744 | bytes 37946536 | solution.py:168
  812.0 7.5 fusion.47
  822.7 12.8 %slice_bitcast_fusion.8 = (f32[2,1,64,768]{3,1,2,0:T(1,128)S(1)}, f32[2,1,64,768]{3,1,2,0:T(1,128)S(1)}, f32[2,1,64,768]{3,1,2,0:T(1,128)S(1)}, f32[2,1,64,768]{...) fusion(f32[2,1,64,9,768]{4,3,2,0,1:T(8,128)} %reshape.209), kind=kLoop, calls=%fused_computation.38 | loop fusion | bytes 7077888 | tf_op jit(solution)/shard_map/while/body/eval_jaxpr/cond/branch_1_fun/squeeze | solution.py:55
  868.9 34.2 %conditional.6 = (f32[2,1,64,768]{3,1,2,0:T(1,128)}, bf16[2,2,64,768]{3,1,2,0:T(2,128)(2,1)}, bf16[2,128,768]{2,1,0:T(8,128)(2,1)}) conditional(s32[]{:T(128)} %convert_element_type.205, bf16[2,128,768]{2,1,0:T(8,128)(2,1)} %get-tuple-element.928, (pred[]{:T(512)}, s32[]{:T(128)}, f32[2,128,768]{2,1,0:T(8,128)}, bf16[768,150]{1,0:T(8,128)(2,1)}, ...), branch_computations={%region_5.5_spmd, %region_6.7_spmd} | conditional | flops 1422863744 | bytes 37946536 | solution.py:168
  873.3 7.5 fusion.47
  884.0 12.8 %slice_bitcast_fusion.8 = (f32[2,1,64,768]{3,1,2,0:T(1,128)S(1)}, f32[2,1,64,768]{3,1,2,0:T(1,128)S(1)}, f32[2,1,64,768]{3,1,2,0:T(1,128)S(1)}, f32[2,1,64,768]{...) fusion(f32[2,1,64,9,768]{4,3,2,0,1:T(8,128)} %reshape.209), kind=kLoop, calls=%fused_computation.38 | loop fusion | bytes 7077888 | tf_op jit(solution)/shard_map/while/body/eval_jaxpr/cond/branch_1_fun/squeeze | solution.py:55
  926.4 9.1 convolution_convert_fusion
  940.8 94.4 %fusion.4 = bf16[104,768]{1,0:T(8,128)(2,1)S(1)} fusion(bf16[3200,768]{1,0:T(8,128)(2,1)} %convolution_convert_fusion.1), kind=kCustom, calls=%all-reduce-scatter | all-reduce-scatter fusion | flops 2555905 | bytes 5075968
  1048.3 113.6 %reduce-scatter.4.cloned.1.call-done = bf16[216,768]{1,0:T(8,128)(2,1)} async-done(((bf16[6912,768]{1,0:T(8,128)(2,1)}), bf16[216,768]{1,0:T(8,128)(2,1)}) %reduce-scatter.4.cloned.1.call-update) | async-done | bytes 331792 | tf_op jit(solution)/shard_map/reduce_scatter | solution.py:200
  (330 shorter events, 422.6 us)
Async XLA Ops:
  7.2 50.2 %all-gather.4.cloned.1.call-start = ((), (), s32[]{:S(2)}) async-start(), calls=%async_computation.1 | async-start | bytes 7372800 | tf_op jit(solution)/shard_map/all_gather | solution.py:72
  7.9 157.2 %all-gather.6.cloned.1.call-start = ((), (), s32[]{:S(2)}) async-start(), calls=%async_computation.3 | async-start | bytes 10137600 | tf_op jit(solution)/shard_map/all_gather | solution.py:78
  9.9 1152.1 %reduce-scatter.4.cloned.1.call-start = ((), (), s32[]{:S(2)}) async-start(), calls=%async_computation.2 | async-start | bytes 10948608 | tf_op jit(solution)/shard_map/reduce_scatter | solution.py:200
  174.8 9.7 collective-permute-start.2
  196.2 11.2 collective-permute-start.2
  198.5 10.7 collective-permute-start.1
  220.8 11.0 collective-permute-start.2
  222.8 10.8 collective-permute-start.1
  234.4 10.8 collective-permute-start
  245.2 9.8 collective-permute-start.2
  263.4 9.8 collective-permute-start.2
  275.4 14.3 %collective-permute-start = (bf16[128,768]{1,0:T(8,128)(2,1)}, bf16[128,768]{1,0:T(8,128)(2,1)S(1)}, u32[]{:S(2)}, u32[]{:S(2)}) collective-permute-start(bf16[128,768]{1,0:T(8,128)(2,1)} %get-tuple-element.891), channel_id=1, source_target_pairs={{0,1},{1,2},{2,3},{3,4},{4,5},{5,6},{6,7},{8,9},{9,10},{10,11},{11... | collective-permute-start | bytes 589832 | tf_op jit(solution)/shard_map/while/body/eval_jaxpr/ppermute | solution.py:27
  289.8 9.8 collective-permute-start.2
  309.4 9.8 collective-permute-start.2
  329.9 9.8 collective-permute-start.2
  349.5 9.8 collective-permute-start.2
  377.2 11.5 collective-permute-start.4
  383.4 11.8 %collective-permute-start.5 = (bf16[2,1,64,768]{3,1,2,0:T(2,128)(2,1)S(1)}, bf16[2,1,64,768]{3,1,2,0:T(2,128)(2,1)S(1)}, u32[]{:S(2)}, u32[]{:S(2)}) collective-permute-start(bf16[2,1,64,768]{3,1,2,0:T(2,128)(2,1)S(1)} %get-tuple-element.865), channel_id=1, source_target_pairs={{0,8},{8,16},{16,24},{24,32},{32,40},{40,48},{48,56},{56,64},{64,7... | collective-permute-start | bytes 589832 | tf_op jit(solution)/shard_map/while/body/eval_jaxpr/ppermute | solution.py:18
  413.0 11.8 %collective-permute-start.5 = (bf16[2,1,64,768]{3,1,2,0:T(2,128)(2,1)S(1)}, bf16[2,1,64,768]{3,1,2,0:T(2,128)(2,1)S(1)}, u32[]{:S(2)}, u32[]{:S(2)}) collective-permute-start(bf16[2,1,64,768]{3,1,2,0:T(2,128)(2,1)S(1)} %get-tuple-element.865), channel_id=1, source_target_pairs={{0,8},{8,16},{16,24},{24,32},{32,40},{40,48},{48,56},{56,64},{64,7... | collective-permute-start | bytes 589832 | tf_op jit(solution)/shard_map/while/body/eval_jaxpr/ppermute | solution.py:18
  441.2 9.7 collective-permute-start.4
  443.2 11.8 %collective-permute-start.5 = (bf16[2,1,64,768]{3,1,2,0:T(2,128)(2,1)S(1)}, bf16[2,1,64,768]{3,1,2,0:T(2,128)(2,1)S(1)}, u32[]{:S(2)}, u32[]{:S(2)}) collective-permute-start(bf16[2,1,64,768]{3,1,2,0:T(2,128)(2,1)S(1)} %get-tuple-element.865), channel_id=1, source_target_pairs={{0,8},{8,16},{16,24},{24,32},{32,40},{40,48},{48,56},{56,64},{64,7... | collective-permute-start | bytes 589832 | tf_op jit(solution)/shard_map/while/body/eval_jaxpr/ppermute | solution.py:18
  472.7 11.8 %collective-permute-start.5 = (bf16[2,1,64,768]{3,1,2,0:T(2,128)(2,1)S(1)}, bf16[2,1,64,768]{3,1,2,0:T(2,128)(2,1)S(1)}, u32[]{:S(2)}, u32[]{:S(2)}) collective-permute-start(bf16[2,1,64,768]{3,1,2,0:T(2,128)(2,1)S(1)} %get-tuple-element.865), channel_id=1, source_target_pairs={{0,8},{8,16},{16,24},{24,32},{32,40},{40,48},{48,56},{56,64},{64,7... | collective-permute-start | bytes 589832 | tf_op jit(solution)/shard_map/while/body/eval_jaxpr/ppermute | solution.py:18
  502.6 11.8 %collective-permute-start.5 = (bf16[2,1,64,768]{3,1,2,0:T(2,128)(2,1)S(1)}, bf16[2,1,64,768]{3,1,2,0:T(2,128)(2,1)S(1)}, u32[]{:S(2)}, u32[]{:S(2)}) collective-permute-start(bf16[2,1,64,768]{3,1,2,0:T(2,128)(2,1)S(1)} %get-tuple-element.865), channel_id=1, source_target_pairs={{0,8},{8,16},{16,24},{24,32},{32,40},{40,48},{48,56},{56,64},{64,7... | collective-permute-start | bytes 589832 | tf_op jit(solution)/shard_map/while/body/eval_jaxpr/ppermute | solution.py:18
  532.2 10.5 collective-permute-start.4
  534.1 12.6 %collective-permute-start.5 = (bf16[2,1,64,768]{3,1,2,0:T(2,128)(2,1)S(1)}, bf16[2,1,64,768]{3,1,2,0:T(2,128)(2,1)S(1)}, u32[]{:S(2)}, u32[]{:S(2)}) collective-permute-start(bf16[2,1,64,768]{3,1,2,0:T(2,128)(2,1)S(1)} %get-tuple-element.865), channel_id=1, source_target_pairs={{0,8},{8,16},{16,24},{24,32},{32,40},{40,48},{48,56},{56,64},{64,7... | collective-permute-start | bytes 589832 | tf_op jit(solution)/shard_map/while/body/eval_jaxpr/ppermute | solution.py:18
  563.2 11.8 %collective-permute-start.5 = (bf16[2,1,64,768]{3,1,2,0:T(2,128)(2,1)S(1)}, bf16[2,1,64,768]{3,1,2,0:T(2,128)(2,1)S(1)}, u32[]{:S(2)}, u32[]{:S(2)}) collective-permute-start(bf16[2,1,64,768]{3,1,2,0:T(2,128)(2,1)S(1)} %get-tuple-element.865), channel_id=1, source_target_pairs={{0,8},{8,16},{16,24},{24,32},{32,40},{40,48},{48,56},{56,64},{64,7... | collective-permute-start | bytes 589832 | tf_op jit(solution)/shard_map/while/body/eval_jaxpr/ppermute | solution.py:18
  579.7 227.9 %collective-permute-start.3 = (bf16[128,768]{1,0:T(8,128)(2,1)S(1)}, bf16[128,768]{1,0:T(8,128)(2,1)S(1)}, u32[]{:S(2)}, u32[]{:S(2)}) collective-permute-start(bf16[128,768]{1,0:T(8,128)(2,1)S(1)} %get-tuple-element.927), channel_id=1, source_target_pairs={{1,0},{2,1},{3,2},{4,3},{5,4},{6,5},{7,6},{9,8},{10,9},{11,10},{12... | collective-permute-start | bytes 589832 | tf_op jit(solution)/shard_map/while/body/eval_jaxpr/ppermute | solution.py:27
  843.6 10.6 collective-permute-start.4
  845.5 12.7 %collective-permute-start.5 = (bf16[2,1,64,768]{3,1,2,0:T(2,128)(2,1)S(1)}, bf16[2,1,64,768]{3,1,2,0:T(2,128)(2,1)S(1)}, u32[]{:S(2)}, u32[]{:S(2)}) collective-permute-start(bf16[2,1,64,768]{3,1,2,0:T(2,128)(2,1)S(1)} %get-tuple-element.865), channel_id=1, source_target_pairs={{0,8},{8,16},{16,24},{24,32},{32,40},{40,48},{48,56},{56,64},{64,7... | collective-permute-start | bytes 589832 | tf_op jit(solution)/shard_map/while/body/eval_jaxpr/ppermute | solution.py:18
  904.9 10.7 collective-permute-start.4
  906.9 14.7 %collective-permute-start.5 = (bf16[2,1,64,768]{3,1,2,0:T(2,128)(2,1)S(1)}, bf16[2,1,64,768]{3,1,2,0:T(2,128)(2,1)S(1)}, u32[]{:S(2)}, u32[]{:S(2)}) collective-permute-start(bf16[2,1,64,768]{3,1,2,0:T(2,128)(2,1)S(1)} %get-tuple-element.865), channel_id=1, source_target_pairs={{0,8},{8,16},{16,24},{24,32},{32,40},{40,48},{48,56},{56,64},{64,7... | collective-permute-start | bytes 589832 | tf_op jit(solution)/shard_map/while/body/eval_jaxpr/ppermute | solution.py:18
  1035.2 11.6 collective-permute-start.6
  (52 other events, 623.2 us)
Sparse Core Ops, SparseCore 0:
  9.9 47.5 all-gather.3
  60.6 104.4 all-gather.5
  935.6 226.2 reduce-scatter.3
where the time goes:
time: 1170 us
  waiting for transfers between devices  668 us (57%)
  starting transfers between devices  196 us (17%)
  local copies, waits for them, and re-layouts  94.6 us (8%)
  blocking collectives  94.4 us (8%)
  matrix products  53 us (5%)
  other arithmetic  48.3 us (4%)
  between operations  14.6 us (1%)
    ppermute x18, waiting for transfers between devices, shifted(): return lax.ppermute(block, axis, route)  286 us
    reduce_scatter x1, waiting for transfers between devices, on_device(): lax.psum_scatter(lax.dot_general(left, grad_pre_rows, (((0,), (0,)), ((),...  114 us
    all_gather x1, waiting for transfers between devices, on_device(): lax.all_gather(lateral_weight[0], 'dp', axis=0, tiled=True)  106 us
    unnamed x1, blocking collectives  94.4 us
    ppermute x18, starting transfers between devices, padded_2(): after = lax.ppermute(initial, axis, down)  77.1 us
    ppermute x18, starting transfers between devices, shifted(): return lax.ppermute(block, axis, route)  63.8 us
    ppermute x18, waiting for transfers between devices, padded_2(): before = lax.ppermute(last, axis, up)  58.3 us
    ppermute x18, starting transfers between devices, padded_2(): before = lax.ppermute(last, axis, up)  51 us
  transfers between devices with their start and end apart: 59, of which 59 were waited for; matrix products, arithmetic and copies ran while one was open for 9% of the time, Pallas kernels for 0%

commit v1 on v0

v1 whole, which is shorter than its diff:
```python
import jax
import jax.numpy as jnp
from jax import lax
from jax.experimental import pallas as pl
from jax.experimental.pallas import tpu as pltpu
from jax.sharding import PartitionSpec as P

MESH = pl.DeviceIdType.MESH
F32 = jnp.float32
BF16 = jnp.bfloat16
NZ = 8
NX = 4
COLS = 64
ROWS = 4
PIX = ROWS * COLS
CH = 768
CK = 256
NCH = CH // CK
KPAD = 112
GROUPS = NX * NZ
KW = KPAD * GROUPS
SECTIONS = 8
CLASSES = 150
CPAD = 256


def nt(a, b):
    return lax.dot_general(a, b, (((1,), (1,)), ((), ())), preferred_element_type=F32)


def tn(a, b):
    return lax.dot_general(a, b, (((0,), (0,)), ((), ())), preferred_element_type=F32)


def nn(a, b):
    return jnp.dot(a, b, preferred_element_type=F32)


def head_kernel(
    taps_hbm, wl_hbm, w_hbm, cls_ref, oh_hbm, conv_out, lat_out,
    taps, wl, w, lateral, ext, xin, xout, gin, gsout, gx, dsilu, acc, gpv, rim_out, rim_in, oh, cg, lg,
    local_sem, tap_send, tap_recv, oh_send, oh_recv, x_send, x_recv, halo_send, halo_recv,
    g_send, g_recv, rim_send, rim_recv, out_sem,
):
    dp = lax.axis_index("dp")
    s = lax.axis_index("section")
    x, z = dp // NZ, dp % NZ
    odd = x % 2
    half = (z % 2 + odd) % 2
    image = z // 2
    has_up = jnp.logical_not(jnp.logical_and(half == 0, x == 0))
    has_down = jnp.logical_not(jnp.logical_and(half == 1, x == NX - 1))
    pair = dp + 1 - 2 * (z % 2)
    up = jnp.where(half == 1, pair, dp - NZ)
    down = jnp.where(half == 0, pair, dp + NZ)
    src_half = z // 4
    is_first, is_last = s == 0, s == SECTIONS - 1

    def home(img):
        return x * NZ + 2 * img + (src_half + odd) % 2

    my_tile = s // 4
    tap_slot = (z % 4) * 4 + s % 4

    wl_copy = pltpu.make_async_copy(wl_hbm, wl, local_sem.at[0])
    w_copy = pltpu.make_async_copy(w_hbm, w, local_sem.at[1])
    wl_copy.start()
    w_copy.start()

    barrier = pltpu.get_barrier_semaphore()

    def greet(d, sec):
        pl.semaphore_signal(barrier, inc=1, device_id={"dp": d, "section": sec}, device_id_type=MESH)

    def tap_source(j):
        return x * NZ + half * 4 + j // 4, (image % 2) * 4 + j % 4

    for j in range(16):
        d, sec = tap_source(j)

        @pl.when(jnp.logical_or(d != dp, sec != s))
        def _():
            greet(d, sec)

    @pl.when(has_up)
    def _():
        greet(up, s)

    @pl.when(has_down)
    def _():
        greet(down, s)

    @pl.when(s > 0)
    def _():
        greet(dp, s - 1)

    @pl.when(s < SECTIONS - 1)
    def _():
        greet(dp, s + 1)

    @pl.when(is_last)
    def _():
        for j in range(4):
            d = x * NZ + half * 4 + j

            @pl.when(d != dp)
            def _():
                greet(d, s)

    def tap_target(k):
        level, micro, core = k // 4, (k // 2) % 2, k % 2
        return home(2 * micro + my_tile), 2 * level + core

    need = jnp.int32(0)
    for k in range(16):
        d, sec = tap_target(k)
        need += jnp.logical_or(d != dp, sec != s).astype(jnp.int32)
    for flag in (has_up, has_down, s > 0, s < SECTIONS - 1):
        need += flag.astype(jnp.int32)
    for img in range(4):
        need += jnp.logical_and(is_last, home(img) != dp).astype(jnp.int32)
    pl.semaphore_wait(barrier, need)

    def tap_rows(j):
        return taps.at[pl.ds(pl.multiple_of((j // 4) * COLS + (j % 4) * 16, 16), 16), :]

    def tap_copy(k):
        d, sec = tap_target(k)
        return pltpu.make_async_remote_copy(
            src_ref=taps_hbm.at[k // 2], dst_ref=tap_rows(tap_slot),
            send_sem=tap_send.at[k], recv_sem=tap_recv.at[tap_slot],
            device_id={"dp": d, "section": sec}, device_id_type=MESH,
        )

    def tap_local(k):
        return pltpu.make_async_copy(taps_hbm.at[k // 2], tap_rows(tap_slot), tap_recv.at[tap_slot])

    for k in range(16):
        d, sec = tap_target(k)
        other = jnp.logical_or(d != dp, sec != s)

        @pl.when(other)
        def _():
            tap_copy(k).start()

        @pl.when(jnp.logical_not(other))
        def _():
            tap_local(k).start()

    def oh_rows(r):
        return oh.at[pl.ds(pl.multiple_of(r * COLS, COLS), COLS), :]

    def oh_src(img):
        return oh_hbm.at[img // 2, pl.ds((img % 2) * COLS, COLS), :]

    def oh_copy(img):
        return pltpu.make_async_remote_copy(
            src_ref=oh_src(img), dst_ref=oh_rows(z % 4),
            send_sem=oh_send.at[img], recv_sem=oh_recv.at[z % 4],
            device_id={"dp": home(img), "section": s}, device_id_type=MESH,
        )

    @pl.when(is_last)
    def _():
        for img in range(4):
            @pl.when(home(img) != dp)
            def _():
                oh_copy(img).start()

            @pl.when(home(img) == dp)
            def _():
                pltpu.make_async_copy(oh_src(img), oh_rows(z % 4), oh_recv.at[z % 4]).start()

    @pl.when(jnp.logical_not(has_up))
    def _():
        ext[0:COLS, :] = jnp.zeros((COLS, CH), BF16)

    @pl.when(jnp.logical_not(has_down))
    def _():
        ext[COLS + PIX:, :] = jnp.zeros((COLS, CH), BF16)

    for j in range(16):
        pltpu.make_async_copy(tap_rows(j), tap_rows(j), tap_recv.at[j]).wait()
    wl_copy.wait()

    for n in range(NCH):
        lateral[:, n * CK:(n + 1) * CK] = nn(taps[...], wl[:, n * CK:(n + 1) * CK])
    w_copy.wait()

    def lanes(c):
        return pl.ds(c * CK, CK)

    def x_copy(c):
        return pltpu.make_async_remote_copy(
            src_ref=xout.at[:, lanes(c)], dst_ref=xin.at[:, lanes(c)],
            send_sem=x_send.at[c], recv_sem=x_recv.at[c],
            device_id={"dp": dp, "section": s + 1}, device_id_type=MESH,
        )

    def halo_up(c):
        return pltpu.make_async_remote_copy(
            src_ref=ext.at[pl.ds(COLS, COLS), lanes(c)], dst_ref=ext.at[pl.ds(COLS + PIX, COLS), lanes(c)],
            send_sem=halo_send.at[0, c], recv_sem=halo_recv.at[1, c],
            device_id={"dp": up, "section": s}, device_id_type=MESH,
        )

    def halo_down(c):
        return pltpu.make_async_remote_copy(
            src_ref=ext.at[pl.ds(PIX, COLS), lanes(c)], dst_ref=ext.at[pl.ds(0, COLS), lanes(c)],
            send_sem=halo_send.at[1, c], recv_sem=halo_recv.at[0, c],
            device_id={"dp": down, "section": s}, device_id_type=MESH,
        )

    def local_wait(ref, sem):
        pltpu.make_async_copy(ref, ref, sem).wait()

    def take_x(c):
        cols = slice(c * CK, (c + 1) * CK)

        @pl.when(is_first)
        def _():
            ext[COLS:COLS + PIX, cols] = lateral[:, cols].astype(BF16)

        @pl.when(s > 0)
        def _():
            local_wait(xin.at[:, lanes(c)], x_recv.at[c])
            ext[COLS:COLS + PIX, cols] = (xin[:, cols].astype(F32) + lateral[:, cols]).astype(BF16)

        @pl.when(has_up)
        def _():
            halo_up(c).start()

        @pl.when(has_down)
        def _():
            halo_down(c).start()

    def wait_halo(c):
        @pl.when(has_up)
        def _():
            local_wait(ext.at[pl.ds(0, COLS), lanes(c)], halo_recv.at[0, c])

        @pl.when(has_down)
        def _():
            local_wait(ext.at[pl.ds(COLS + PIX, COLS), lanes(c)], halo_recv.at[1, c])

    def conv_part(c, dr, dc, ncols):
        rows = (1 + dr) * COLS
        return nn(
            ext[rows:rows + PIX, c * CK:(c + 1) * CK],
            w[(dr + 1) * 3 + dc + 1, c * CK:(c + 1) * CK, ncols],
        )

    every = slice(0, CH)

    def conv_inner(c, start):
        for dc in (-1, 0, 1):
            term = conv_part(c, 0, dc, every)
            if start:
                acc[dc + 1] = term
            else:
                acc[dc + 1] += term

    def conv_outer(c):
        for dc in (-1, 0, 1):
            acc[dc + 1] += conv_part(c, -1, dc, every) + conv_part(c, 1, dc, every)

    col = lax.broadcasted_iota(jnp.int32, (PIX, CK), 0) % COLS

    def before(v):
        return jnp.where(col == 0, 0.0, pltpu.roll(v, 1, 0))

    def after(v):
        return jnp.where(col == COLS - 1, 0.0, pltpu.roll(v, PIX - 1, 0))

    take_x(0)
    take_x(1)
    conv_inner(0, True)
    wait_halo(0)
    conv_outer(0)
    take_x(2)
    conv_inner(1, False)
    conv_inner(2, False)
    wait_halo(1)
    conv_outer(1)
    wait_halo(2)
    for n in range(NCH):
        ncols = slice(n * CK, (n + 1) * CK)
        parts = [
            acc[dc + 1, :, ncols] + conv_part(2, -1, dc, ncols) + conv_part(2, 1, dc, ncols)
            for dc in (-1, 0, 1)
        ]
        pre = before(parts[0]) + parts[1] + after(parts[2])
        sig = 1.0 / (1.0 + jnp.exp(-pre))
        xout[:, ncols] = (pre * sig).astype(BF16)

        @pl.when(s < SECTIONS - 1)
        def _():
            x_copy(n).start()

        dsilu[:, ncols] = sig * (1.0 + pre * (1.0 - sig))

    @pl.when(is_last)
    def _():
        for r in range(4):
            local_wait(oh_rows(r), oh_recv.at[r])
        logits = nn(xout[...], cls_ref[...])
        lane = lax.broadcasted_iota(jnp.int32, (PIX, CPAD), 1)
        real = lane < CLASSES
        expo = jnp.where(real, jnp.exp(logits), 0.0)
        probs = expo / jnp.sum(expo, axis=-1, keepdims=True)
        marks = oh[...].astype(F32)
        weight = jnp.sum(jnp.where(lane == CPAD - 1, marks, 0.0), axis=-1, keepdims=True)
        hot = jnp.where(real, marks, 0.0)
        grad_logits = ((probs - hot) * weight).astype(BF16)
        gx[...] = nt(grad_logits, cls_ref[...])

    def g_copy(c):
        return pltpu.make_async_remote_copy(
            src_ref=gsout.at[:, lanes(c)], dst_ref=gin.at[:, lanes(c)],
            send_sem=g_send.at[c], recv_sem=g_recv.at[c],
            device_id={"dp": dp, "section": s - 1}, device_id_type=MESH,
        )

    def rim_up(c):
        return pltpu.make_async_remote_copy(
            src_ref=rim_out.at[0, :, lanes(c)], dst_ref=rim_in.at[1, :, lanes(c)],
            send_sem=rim_send.at[0, c], recv_sem=rim_recv.at[1, c],
            device_id={"dp": up, "section": s}, device_id_type=MESH,
        )

    def rim_down(c):
        return pltpu.make_async_remote_copy(
            src_ref=rim_out.at[1, :, lanes(c)], dst_ref=rim_in.at[0, :, lanes(c)],
            send_sem=rim_send.at[1, c], recv_sem=rim_recv.at[0, c],
            device_id={"dp": down, "section": s}, device_id_type=MESH,
        )

    def take_g(c):
        cols = slice(c * CK, (c + 1) * CK)

        @pl.when(s < SECTIONS - 1)
        def _():
            local_wait(gin.at[:, lanes(c)], g_recv.at[c])
            gx[:, cols] = gin[:, cols].astype(F32)

        grad_pre = (gx[:, cols] * dsilu[:, cols]).astype(BF16).astype(F32)
        gpv[0, :, cols] = after(grad_pre).astype(BF16)
        gpv[1, :, cols] = grad_pre.astype(BF16)
        gpv[2, :, cols] = before(grad_pre).astype(BF16)

    def back_part(c, dr, krows):
        total = None
        for dc in (-1, 0, 1):
            term = nt(
                gpv[dc + 1, :, c * CK:(c + 1) * CK],
                w[(dr + 1) * 3 + dc + 1, krows, c * CK:(c + 1) * CK],
            )
            total = term if total is None else total + term
        return total

    take_g(0)
    for dr in (-1, 0, 1):
        acc[dr + 1] = back_part(0, dr, every)
    take_g(1)
    for dr in (-1, 0, 1):
        acc[dr + 1] += back_part(1, dr, every)
    take_g(2)
    for n in range(NCH):
        ncols = slice(n * CK, (n + 1) * CK)
        upper = acc[0, :, ncols] + back_part(2, -1, ncols)
        acc[0, :, ncols] = upper
        rim_out[0, :, ncols] = upper[0:COLS].astype(BF16)
        lower = acc[2, :, ncols] + back_part(2, 1, ncols)
        acc[2, :, ncols] = lower
        rim_out[1, :, ncols] = lower[PIX - COLS:].astype(BF16)

        @pl.when(has_up)
        def _():
            rim_up(n).start()

        @pl.when(has_down)
        def _():
            rim_down(n).start()

    acc[1] += back_part(2, 0, every)
    for n in range(NCH):
        ncols = slice(n * CK, (n + 1) * CK)
        acc[1, 0:PIX - COLS, ncols] += acc[0, COLS:, ncols]
        acc[1, COLS:, ncols] += acc[2, 0:PIX - COLS, ncols]

        @pl.when(has_up)
        def _():
            local_wait(rim_in.at[0, :, lanes(n)], rim_recv.at[0, n])
            acc[1, 0:COLS, ncols] += rim_in[0, :, ncols].astype(F32)

        @pl.when(has_down)
        def _():
            local_wait(rim_in.at[1, :, lanes(n)], rim_recv.at[1, n])
            acc[1, PIX - COLS:, ncols] += rim_in[1, :, ncols].astype(F32)

        gsout[:, ncols] = acc[1, :, ncols].astype(BF16)

        @pl.when(s > 0)
        def _():
            g_copy(n).start()

    def conv_grad_copy(o):
        return pltpu.make_async_copy(cg.at[o], conv_out.at[o], out_sem.at[o])

    for dr in (-1, 0, 1):
        rows = (1 + dr) * COLS
        flipped = ext[rows:rows + PIX, :].T
        for dc in (-1, 0, 1):
            o = (dr + 1) * 3 + dc + 1
            cg[o] = nn(flipped, gpv[dc + 1]).astype(BF16)
            conv_grad_copy(o).start()

    lat_copy = pltpu.make_async_copy(lg, lat_out, out_sem.at[9])

    @pl.loop(0, KW // 512)
    def _(b):
        at = pl.ds(pl.multiple_of(b * 512, 512), 512)
        lg[at, :] = nn(taps[:, at].T, gsout[...]).astype(BF16)

    lat_copy.start()

    for k in range(16):
        d, sec = tap_target(k)

        @pl.when(jnp.logical_or(d != dp, sec != s))
        def _():
            tap_copy(k).wait_send()

    @pl.when(is_last)
    def _():
        for img in range(4):
            @pl.when(home(img) != dp)
            def _():
                oh_copy(img).wait_send()

    for c in range(NCH):
        @pl.when(s < SECTIONS - 1)
        def _():
            x_copy(c).wait_send()

        @pl.when(s > 0)
        def _():
            g_copy(c).wait_send()

        @pl.when(has_up)
        def _():
            halo_up(c).wait_send()
            rim_up(c).wait_send()

        @pl.when(has_down)
        def _():
            halo_down(c).wait_send()
            rim_down(c).wait_send()

    for o in range(9):
        conv_grad_copy(o).wait()
    lat_copy.wait()


def head_call(taps, wl, w, cls, oh):
    dma = pltpu.SemaphoreType.DMA
    hbm = pl.BlockSpec(memory_space=pl.ANY)
    vmem = pl.BlockSpec(memory_space=pltpu.VMEM)
    return pl.pallas_call(
        head_kernel,
        out_shape=(
            jax.ShapeDtypeStruct((9, CH, CH), BF16),
            jax.ShapeDtypeStruct((KW, CH), BF16),
        ),
        in_specs=[hbm, hbm, hbm, vmem, hbm],
        out_specs=(hbm, hbm),
        scratch_shapes=[
            pltpu.VMEM((PIX, KW), BF16),
            pltpu.VMEM((KW, CH), BF16),
            pltpu.VMEM((9, CH, CH), BF16),
            pltpu.VMEM((PIX, CH), F32),
            pltpu.VMEM((PIX + 2 * COLS, CH), BF16),
            pltpu.VMEM((PIX, CH), BF16),
            pltpu.VMEM((PIX, CH), BF16),
            pltpu.VMEM((PIX, CH), BF16),
            pltpu.VMEM((PIX, CH), BF16),
            pltpu.VMEM((PIX, CH), F32),
            pltpu.VMEM((PIX, CH), F32),
            pltpu.VMEM((3, PIX, CH), F32),
            pltpu.VMEM((3, PIX, CH), BF16),
            pltpu.VMEM((2, COLS, CH), BF16),
            pltpu.VMEM((2, COLS, CH), BF16),
            pltpu.VMEM((PIX, CPAD), BF16),
            pltpu.VMEM((9, CH, CH), BF16),
            pltpu.VMEM((KW, CH), BF16),
            dma((2,)),
            dma((16,)),
            dma((16,)),
            dma((4,)),
            dma((4,)),
            dma((NCH,)),
            dma((NCH,)),
            dma((2, NCH)),
            dma((2, NCH)),
            dma((NCH,)),
            dma((NCH,)),
            dma((2, NCH)),
            dma((2, NCH)),
            dma((10,)),
        ],
        compiler_params=pltpu.CompilerParams(
            collective_id=0, has_side_effects=True, vmem_limit_bytes=56 << 20
        ),
    )(taps, wl, w, cls, oh)


def on_device(tap_maps, lateral_weight, conv_weight, classifier, tile_counts, labels):
    levels, micros, here, width = tap_maps.shape
    per = width // GROUPS
    classes = classifier.shape[1]
    pixels = labels.shape[1]
    grouped = tap_maps.reshape(levels * micros, here, GROUPS, per)
    taps = jnp.pad(grouped, ((0, 0), (0, 0), (0, 0), (0, KPAD - per))).reshape(levels * micros, here, KW)
    own = jnp.pad(lateral_weight[0], ((0, KPAD - per), (0, 0)))
    wl = lax.all_gather(own, "dp", axis=0, tiled=True)
    cls = jnp.pad(classifier, ((0, 0), (0, CPAD - classes)))
    counts = tile_counts[0][:, None]
    valid = (jnp.arange(pixels)[None, :] // COLS < counts).astype(F32)
    weight = valid / (counts.astype(F32) * COLS * GROUPS * micros)
    lane = jnp.arange(CPAD)
    hot = (labels[:, :, None] == lane).astype(F32)
    oh = jnp.where(lane == CPAD - 1, weight[:, :, None], hot).astype(BF16)
    conv_part, lat_part = head_call(taps, wl, conv_weight.reshape(9, CH, CH), cls, oh)
    conv_grad = lax.psum_scatter(
        conv_part.reshape(9 * CH, CH), "dp", scatter_dimension=0, tiled=True
    ).astype(F32)
    lateral_grad = lax.psum_scatter(lat_part, "dp", scatter_dimension=0, tiled=True)[:per].astype(F32)
    return (conv_grad[None], lateral_grad[None])


def solution(mesh):
    placed = (
        P(None, None, ("dp", "section"), None),
        P("section", "dp", None),
        P("section", None, None),
        P(),
        P("dp", None),
        P(None, "dp"),
    )
    return jax.shard_map(
        on_device,
        mesh=mesh,
        in_specs=placed,
        out_specs=(P("section", "dp", None), P("section", "dp", None)),
        check_vma=False,
    )
```

time: 1170 us -> 800 us (0.68)
  Pallas kernels: 0 us -> 224 us
  starting transfers between devices: 196 us -> 0.12 us
  waiting for transfers between devices: 668 us -> 542 us
  blocking collectives: 94.4 us -> 0 us
  local copies, waits for them, and re-layouts: 94.6 us -> 13.1 us
  matrix products: 53 us -> 0 us
  other arithmetic: 48.3 us -> 5.67 us
    ppermute x54 -> x0, waiting for transfers between devices: 394 us -> none  [the longest x18 286 us: shifted(): return lax.ppermute(block, axis, route)]
    reduce_scatter x1 -> x2, waiting for transfers between devices: 114 us -> 465 us  [the longest x1 237 us: on_device(): lax.psum_scatter(lat_part, 'dp', scatter_dimension=0, tiled=True)[:per]]
    pallas_call x0 -> x1, Pallas kernels: none -> 224 us  [head_call(): pl.pallas_call(head_kernel, out_shape=(jax.ShapeDtypeStruct((9, CH, CH),...]
    ppermute x54 -> x0, starting transfers between devices: 192 us -> none  [the longest x18 77.1 us: padded_2(): after = lax.ppermute(initial, axis, down)]
    unnamed x1 -> x0, blocking collectives: 94.4 us -> none
    all_gather x2 -> x1, waiting for transfers between devices: 153 us -> 76.5 us  [on_device(): wl = lax.all_gather(own, 'dp', axis=0, tiled=True)]
    dot_general x11 -> x0, matrix products: 53 us -> none  [the longest x2 15 us: backward_advance(): lax.dot_general(grad_pre, weights, (((1,), (1,)), ((), ())), preferred_el...]
    convert_element_type x27 -> x1, other arithmetic: 36 us -> 1.49 us  [on_device(): oh = jnp.where(lane == CPAD - 1, weight[:, :, None], hot).astype(BF16)]
  transfers between devices with their start and end apart: 59 -> 3, of which waited for: 59 -> 3; matrix products, arithmetic and copies ran while one was open for 9% -> 2% of each run, Pallas kernels for 0% -> 0%
where the time goes in v1:
time: 800 us; the launch traced here: 799 us
  waiting for transfers between devices  542 us (68%)
  Pallas kernels  224 us (28%)
  between operations  13.8 us (2%)
  local copies, waits for them, and re-layouts  13.1 us (2%)
    reduce_scatter x1, waiting for transfers between devices, on_device(): lax.psum_scatter(lat_part, 'dp', scatter_dimension=0, tiled=True)[:per]  237 us
    reduce_scatter x1, waiting for transfers between devices, on_device(): lax.psum_scatter(conv_part.reshape(9 * CH, CH), 'dp', scatter_dimension=0...  227 us
    pallas_call x1, Pallas kernels, head_call(): pl.pallas_call(head_kernel, out_shape=(jax.ShapeDtypeStruct((9, CH, CH),...  224 us
    all_gather x1, waiting for transfers between devices, on_device(): wl = lax.all_gather(own, 'dp', axis=0, tiled=True)  76.5 us
  transfers between devices with their start and end apart: 3, of which 3 were waited for; matrix products, arithmetic and copies ran while one was open for 2% of the time, Pallas kernels for 0%

profile of v1, /device:TPU:2, one launch (start us, length us, event | category | flops | bytes accessed | tf_op | source)
XLA Modules:
  0.0 799.1 jit_solution(4876108214777968534)
XLA Ops:
  7.2 0.0 all-gather.2.cloned.1.call-start
  7.2 1.6 pad.13
  8.8 0.0 all-gather.2.cloned.1.call-update
  8.8 0.0 reduce-scatter.5.cloned.1.call-start
  8.9 1.1 copy.8
  10.0 0.8 pad.14.cls_ref
  10.8 5.1 reshape.111
  15.9 0.3 pad.12
  16.1 3.2 reshape.112.taps_hbm
  19.4 0.7 convert_multiply_fusion
  20.0 0.7 fusion.1
  20.7 1.5 select_convert_fusion.oh_hbm
  22.2 76.5 %all-gather.2.cloned.1.call-done.wl_hbm = bf16[3584,768]{1,0:T(8,128)(2,1)} async-done(((bf16[112,768]{1,0:T(8,128)(2,1)}), bf16[3584,768]{1,0:T(8,128)(2,1)}) %all-gather.2.cloned.1.call-update) | async-done | bytes 5505040 | tf_op jit(solution)/shard_map/all_gather | solution.py:525
  98.8 224.3 %shard_map.77 = (bf16[9,768,768]{2,1,0:T(8,128)(2,1)}, bf16[3584,768]{1,0:T(8,128)(2,1)}) custom-call(bf16[8,16,3584]{2,1,0:T(8,128)(2,1)} %reshape.112.taps_hbm, bf16[3584,768]{1,0:T(8,128)(2,1)} %all-gather.2.cloned.1.call-done.wl_hbm, bf16[9,768,768]{2,1,0:T(8,128)(2,1)} %bitcast.17, bf16[768,256]{1,0:T(8,128)(2,1)} %pad.14.cls_ref, ...), custom_call_target="tpu_custom_call" | custom-call | tf_op jit(solution)/shard_map/pallas_call | solution.py:469
  323.1 0.0 reduce-scatter.5.cloned.1.call-update
  323.2 0.0 reduce-scatter.3.cloned.1.call-start
  323.2 0.7 reduce-scatter.3.cloned.1.call-update
  323.9 237.4 %reduce-scatter.5.cloned.1.call-done = bf16[112,768]{1,0:T(8,128)(2,1)} async-done(((bf16[3584,768]{1,0:T(8,128)(2,1)}), bf16[112,768]{1,0:T(8,128)(2,1)}) %reduce-scatter.5.cloned.1.call-update) | async-done | bytes 172048 | tf_op jit(solution)/shard_map/reduce_scatter | solution.py:537
  561.3 0.9 fusion
  562.2 1.0 copy.9
  563.2 227.5 %reduce-scatter.3.cloned.1.call-done = bf16[216,768]{1,0:T(8,128)(2,1)} async-done(((bf16[6912,768]{1,0:T(8,128)(2,1)}), bf16[216,768]{1,0:T(8,128)(2,1)}) %reduce-scatter.3.cloned.1.call-update) | async-done | bytes 331792 | tf_op jit(solution)/shard_map/reduce_scatter | solution.py:534
  790.7 1.9 bitcast_convert_fusion
  (2 shorter events, 0.0 us)
Async XLA Ops:
  7.2 91.6 %all-gather.2.cloned.1.call-start = ((), (), s32[]{:S(2)}) async-start(), calls=%async_computation.2 | async-start | bytes 5677056 | tf_op jit(solution)/shard_map/all_gather | solution.py:525
  8.8 552.4 %reduce-scatter.5.cloned.1.call-start = ((), (), s32[]{:S(2)}) async-start(), calls=%async_computation.4 | async-start | bytes 5677056 | tf_op jit(solution)/shard_map/reduce_scatter | solution.py:537
  323.2 467.5 %reduce-scatter.3.cloned.1.call-start = ((), (), s32[]{:S(2)}) async-start(), calls=%async_computation.3 | async-start | bytes 10948608 | tf_op jit(solution)/shard_map/reduce_scatter | solution.py:534
Sparse Core Ops, SparseCore 0:
  11.2 87.5 all-gather.1
  323.3 237.9 reduce-scatter.4
  565.5 225.1 reduce-scatter.2

commit v2 on v1

--- a/solution.py
+++ b/solution.py
@@ -20,6 +20,11 @@
 GROUPS = NX * NZ
 KW = KPAD * GROUPS
 SECTIONS = 8
+WIDE = NX * PIX
+CROWS = 9 * CH // GROUPS
+XC, XL = CROWS * NZ, KPAD * NZ
+UNIT = XC // 9
+HALF = CH // 2
 CLASSES = 150
 CPAD = 256
 
@@ -38,9 +43,10 @@
 
 def head_kernel(
     taps_hbm, wl_hbm, w_hbm, cls_ref, oh_hbm, conv_out, lat_out,
-    taps, wl, w, lateral, ext, xin, xout, gin, gsout, gx, dsilu, acc, gpv, rim_out, rim_in, oh, cg, lg,
+    taps, wl, w, lateral, ext, xin, xout, gin, dsilu, acc, gpv, rim_out, rim_in, oh,
+    ext_all, taps_all, gp_all, gs_all, gpv_all, cols_t, taps_t, part_c, part_l, ring_c, ring_l,
     local_sem, tap_send, tap_recv, oh_send, oh_recv, x_send, x_recv, halo_send, halo_recv,
-    g_send, g_recv, rim_send, rim_recv, out_sem,
+    g_send, g_recv, rim_send, rim_recv, early_sem, e_send, e_recv, a_send, a_recv, rc_send, rc_recv, rl_send, rl_recv,
 ):
     dp = lax.axis_index("dp")
     s = lax.axis_index("section")
@@ -59,6 +65,10 @@
     def home(img):
         return x * NZ + 2 * img + (src_half + odd) % 2
 
+    gx = lateral
+    early = s < 4
+    z_next, z_prev = x * NZ + (z + 1) % NZ, x * NZ + (z + NZ - 1) % NZ
+
     my_tile = s // 4
     tap_slot = (z % 4) * 4 + s % 4
 
@@ -82,6 +92,11 @@
         def _():
             greet(d, sec)
 
+    for k in range(1, NX):
+        greet((x + k) % NX * NZ + z, s)
+    greet(z_next, s)
+    greet(z_prev, s)
+
     @pl.when(has_up)
     def _():
         greet(up, s)
@@ -111,7 +126,7 @@
         level, micro, core = k // 4, (k // 2) % 2, k % 2
         return home(2 * micro + my_tile), 2 * level + core
 
-    need = jnp.int32(0)
+    need = jnp.int32(NX - 1 + 2)
     for k in range(16):
         d, sec = tap_target(k)
         need += jnp.logical_or(d != dp, sec != s).astype(jnp.int32)
@@ -299,6 +314,48 @@
 
         dsilu[:, ncols] = sig * (1.0 + pre * (1.0 - sig))
 
+    def early_copies(k):
+        peer = (x + k) % NX
+        to = {"dp": peer * NZ + z, "section": s}
+        at = pl.ds(pl.multiple_of(peer * XL, 128), XL)
+        return (
+            pltpu.make_async_remote_copy(
+                src_ref=ext, dst_ref=ext_all.at[x], send_sem=e_send.at[0, k], recv_sem=e_recv.at[0, x],
+                device_id=to, device_id_type=MESH,
+            ),
+            pltpu.make_async_remote_copy(
+                src_ref=taps.at[:, at], dst_ref=taps_all.at[x], send_sem=e_send.at[1, k], recv_sem=e_recv.at[1, x],
+                device_id=to, device_id_type=MESH,
+            ),
+        )
+
+    def exchange_early():
+        at = pl.ds(pl.multiple_of(x * XL, 128), XL)
+        pltpu.make_async_copy(ext, ext_all.at[x], e_recv.at[0, x]).start()
+        pltpu.make_async_copy(taps.at[:, at], taps_all.at[x], e_recv.at[1, x]).start()
+        for k in range(1, NX):
+            for copy in early_copies(k):
+                copy.start()
+        for src in range(NX):
+            local_wait(ext_all.at[src], e_recv.at[0, src])
+            local_wait(taps_all.at[src], e_recv.at[1, src])
+            lanes_of = slice(src * PIX, (src + 1) * PIX)
+            for dr in range(3):
+                cols_t[dr, :, lanes_of] = ext_all[src, dr * COLS:dr * COLS + PIX, :].T
+            taps_t[:, lanes_of] = taps_all[src].T
+
+    @pl.when(jnp.logical_and(early, s % 2 == 1))
+    def _():
+        pl.semaphore_signal(early_sem, inc=1, device_id={"dp": dp, "section": s - 1}, device_id_type=MESH)
+
+    @pl.when(jnp.logical_and(early, s % 2 == 0))
+    def _():
+        pl.semaphore_wait(early_sem, 1)
+
+    @pl.when(early)
+    def _():
+        exchange_early()
+
     @pl.when(is_last)
     def _():
         for r in range(4):
@@ -316,7 +373,7 @@
 
     def g_copy(c):
         return pltpu.make_async_remote_copy(
-            src_ref=gsout.at[:, lanes(c)], dst_ref=gin.at[:, lanes(c)],
+            src_ref=gs_all.at[x, :, lanes(c)], dst_ref=gin.at[:, lanes(c)],
             send_sem=g_send.at[c], recv_sem=g_recv.at[c],
             device_id={"dp": dp, "section": s - 1}, device_id_type=MESH,
         )
@@ -346,6 +403,7 @@
         grad_pre = (gx[:, cols] * dsilu[:, cols]).astype(BF16).astype(F32)
         gpv[0, :, cols] = after(grad_pre).astype(BF16)
         gpv[1, :, cols] = grad_pre.astype(BF16)
+        gp_all[x, :, cols] = grad_pre.astype(BF16)
         gpv[2, :, cols] = before(grad_pre).astype(BF16)
 
     def back_part(c, dr, krows):
@@ -398,31 +456,89 @@
             local_wait(rim_in.at[1, :, lanes(n)], rim_recv.at[1, n])
             acc[1, PIX - COLS:, ncols] += rim_in[1, :, ncols].astype(F32)
 
-        gsout[:, ncols] = acc[1, :, ncols].astype(BF16)
+        gs_all[x, :, ncols] = acc[1, :, ncols].astype(BF16)
 
         @pl.when(s > 0)
         def _():
             g_copy(n).start()
 
-    def conv_grad_copy(o):
-        return pltpu.make_async_copy(cg.at[o], conv_out.at[o], out_sem.at[o])
-
-    for dr in (-1, 0, 1):
-        rows = (1 + dr) * COLS
-        flipped = ext[rows:rows + PIX, :].T
-        for dc in (-1, 0, 1):
-            o = (dr + 1) * 3 + dc + 1
-            cg[o] = nn(flipped, gpv[dc + 1]).astype(BF16)
-            conv_grad_copy(o).start()
-
-    lat_copy = pltpu.make_async_copy(lg, lat_out, out_sem.at[9])
-
-    @pl.loop(0, KW // 512)
-    def _(b):
-        at = pl.ds(pl.multiple_of(b * 512, 512), 512)
-        lg[at, :] = nn(taps[:, at].T, gsout[...]).astype(BF16)
-
-    lat_copy.start()
+    def ring_copy(kind, k):
+        ref = (gp_all, gs_all)[kind]
+        return pltpu.make_async_remote_copy(
+            src_ref=ref.at[x], dst_ref=ref.at[x], send_sem=a_send.at[kind, k], recv_sem=a_recv.at[kind, x],
+            device_id={"dp": (x + k) % NX * NZ + z, "section": s}, device_id_type=MESH,
+        )
+
+    for kind in range(2):
+        for k in range(1, NX):
+            ring_copy(kind, k).start()
+
+    @pl.when(jnp.logical_not(early))
+    def _():
+        exchange_early()
+
+    def wait_ring(kind, src):
+        @pl.when(src != x)
+        def _():
+            local_wait((gp_all, gs_all)[kind].at[src], a_recv.at[kind, src])
+
+    whole_col = lax.broadcasted_iota(jnp.int32, (PIX, CH), 0) % COLS
+    for src in range(NX):
+        wait_ring(0, src)
+        rows = slice(src * PIX, (src + 1) * PIX)
+        value = gp_all[src].astype(F32)
+        gpv_all[0, rows, :] = jnp.where(whole_col == COLS - 1, 0.0, pltpu.roll(value, PIX - 1, 0)).astype(BF16)
+        gpv_all[1, rows, :] = gp_all[src]
+        gpv_all[2, rows, :] = jnp.where(whole_col == 0, 0.0, pltpu.roll(value, 1, 0)).astype(BF16)
+
+    @pl.loop(0, 9)
+    def _(u):
+        unit = 9 * x + u
+        o = unit // 4
+        chans = pl.ds(pl.multiple_of((unit % 4) * UNIT, UNIT), UNIT)
+        part_c[pl.ds(pl.multiple_of(u * UNIT, UNIT), UNIT), :] = nn(cols_t[o // 3, chans, :], gpv_all[o % 3])
+
+    def slice_at(way, t):
+        return (z + NZ - 1 - t) % NZ if way == 0 else (z + 1 + t) % NZ
+
+    def own_rows(part, rows, way, t):
+        at = pl.ds(pl.multiple_of(slice_at(way, t) * rows, 8), rows)
+        return part[at, way * HALF:(way + 1) * HALF]
+
+    def hop(ring, send, recv, way, t):
+        return pltpu.make_async_remote_copy(
+            src_ref=ring.at[way, t], dst_ref=ring.at[way, t + 1],
+            send_sem=send.at[way, t], recv_sem=recv.at[way, t],
+            device_id={"dp": z_next if way == 0 else z_prev, "section": s}, device_id_type=MESH,
+        )
+
+    conv_ring = (ring_c, rc_send, rc_recv)
+    lat_ring = (ring_l, rl_send, rl_recv)
+    for way in range(2):
+        ring_c[way, 0] = own_rows(part_c, CROWS, way, 0).astype(BF16)
+        hop(*conv_ring, way, 0).start()
+
+    for src in range(NX):
+        wait_ring(1, src)
+    spread = gs_all[...].reshape(WIDE, CH)
+
+    part_l[...] = nn(taps_t[...], spread)
+
+    for way in range(2):
+        ring_l[way, 0] = own_rows(part_l, KPAD, way, 0).astype(BF16)
+        hop(*lat_ring, way, 0).start()
+
+    for t in range(NZ - 1):
+        for ring, part, rows, out in ((conv_ring, part_c, CROWS, conv_out), (lat_ring, part_l, KPAD, lat_out)):
+            for way in range(2):
+                buf = ring[0]
+                local_wait(buf.at[way, t + 1], ring[2].at[way, t])
+                total = buf[way, t + 1].astype(F32) + own_rows(part, rows, way, t + 1)
+                if t < NZ - 2:
+                    buf[way, t + 1] = total.astype(BF16)
+                    hop(*ring, way, t + 1).start()
+                else:
+                    out[:, way * HALF:(way + 1) * HALF] = total
 
     for k in range(16):
         d, sec = tap_target(k)
@@ -457,9 +573,15 @@
             halo_down(c).wait_send()
             rim_down(c).wait_send()
 
-    for o in range(9):
-        conv_grad_copy(o).wait()
-    lat_copy.wait()
+    for k in range(1, NX):
+        for copy in early_copies(k):
+            copy.wait_send()
+        for kind in range(2):
+            ring_copy(kind, k).wait_send()
+    for way in range(2):
+        for t in range(NZ - 1):
+            hop(*conv_ring, way, t).wait_send()
+            hop(*lat_ring, way, t).wait_send()
 
 
 def head_call(taps, wl, w, cls, oh):
@@ -469,11 +591,11 @@
     return pl.pallas_call(
         head_kernel,
         out_shape=(
-            jax.ShapeDtypeStruct((9, CH, CH), BF16),
-            jax.ShapeDtypeStruct((KW, CH), BF16),
+            jax.ShapeDtypeStruct((CROWS, CH), F32),
+            jax.ShapeDtypeStruct((KPAD, CH), F32),
         ),
         in_specs=[hbm, hbm, hbm, vmem, hbm],
-        out_specs=(hbm, hbm),
+        out_specs=(vmem, vmem),
         scratch_shapes=[
             pltpu.VMEM((PIX, KW), BF16),
             pltpu.VMEM((KW, CH), BF16),
@@ -483,16 +605,23 @@
             pltpu.VMEM((PIX, CH), BF16),
             pltpu.VMEM((PIX, CH), BF16),
             pltpu.VMEM((PIX, CH), BF16),
-            pltpu.VMEM((PIX, CH), BF16),
-            pltpu.VMEM((PIX, CH), F32),
             pltpu.VMEM((PIX, CH), F32),
             pltpu.VMEM((3, PIX, CH), F32),
             pltpu.VMEM((3, PIX, CH), BF16),
             pltpu.VMEM((2, COLS, CH), BF16),
             pltpu.VMEM((2, COLS, CH), BF16),
             pltpu.VMEM((PIX, CPAD), BF16),
-            pltpu.VMEM((9, CH, CH), BF16),
-            pltpu.VMEM((KW, CH), BF16),
+            pltpu.VMEM((NX, PIX + 2 * COLS, CH), BF16),
+            pltpu.VMEM((NX, PIX, XL), BF16),
+            pltpu.VMEM((NX, PIX, CH), BF16),
+            pltpu.VMEM((NX, PIX, CH), BF16),
+            pltpu.VMEM((3, WIDE, CH), BF16),
+            pltpu.VMEM((3, CH, WIDE), BF16),
+            pltpu.VMEM((XL, WIDE), BF16),
+            pltpu.VMEM((XC, CH), F32),
+            pltpu.VMEM((XL, CH), F32),
+            pltpu.VMEM((2, NZ, CROWS, HALF), BF16),
+            pltpu.VMEM((2, NZ, KPAD, HALF), BF16),
             dma((2,)),
             dma((16,)),
             dma((16,)),
@@ -506,10 +635,18 @@
             dma((NCH,)),
             dma((2, NCH)),
             dma((2, NCH)),
-            dma((10,)),
+            pltpu.SemaphoreType.REGULAR,
+            dma((2, NX)),
+            dma((2, NX)),
+            dma((2, NX)),
+            dma((2, NX)),
+            dma((2, NZ - 1)),
+            dma((2, NZ - 1)),
+            dma((2, NZ - 1)),
+            dma((2, NZ - 1)),
         ],
         compiler_params=pltpu.CompilerParams(
-            collective_id=0, has_side_effects=True, vmem_limit_bytes=56 << 20
+            collective_id=0, has_side_effects=True, vmem_limit_bytes=60 << 20
         ),
     )(taps, wl, w, cls, oh)
 
@@ -530,12 +667,8 @@
     lane = jnp.arange(CPAD)
     hot = (labels[:, :, None] == lane).astype(F32)
     oh = jnp.where(lane == CPAD - 1, weight[:, :, None], hot).astype(BF16)
-    conv_part, lat_part = head_call(taps, wl, conv_weight.reshape(9, CH, CH), cls, oh)
-    conv_grad = lax.psum_scatter(
-        conv_part.reshape(9 * CH, CH), "dp", scatter_dimension=0, tiled=True
-    ).astype(F32)
-    lateral_grad = lax.psum_scatter(lat_part, "dp", scatter_dimension=0, tiled=True)[:per].astype(F32)
-    return (conv_grad[None], lateral_grad[None])
+    conv_grad, lateral_grad = head_call(taps, wl, conv_weight.reshape(9, CH, CH), cls, oh)
+    return (conv_grad[None], lateral_grad[None, :per])
 
 
 def solution(mesh):

time: 800 us -> 444 us (0.56)
  the two profiles are of different devices: /device:TPU:2 before, /device:TPU:16 now
where the time goes in v2:
time: 444 us; the launch traced here: 443 us
  Pallas kernels  333 us (75%)
  waiting for transfers between devices  77.8 us (18%)
  local copies, waits for them, and re-layouts  16 us (4%)
  between operations  14.1 us (3%)
    pallas_call x1, Pallas kernels, head_call(): pl.pallas_call(head_kernel, out_shape=(jax.ShapeDtypeStruct((CROWS, CH),...  333 us
    all_gather x1, waiting for transfers between devices, on_device(): wl = lax.all_gather(own, 'dp', axis=0, tiled=True)  77.7 us
  transfers between devices with their start and end apart: 1, of which 1 were waited for; matrix products, arithmetic and copies ran while one was open for 3% of the time, Pallas kernels for 0%

profile of v2, /device:TPU:16, one launch (start us, length us, event | category | flops | bytes accessed | tf_op | source)
XLA Modules:
  0.0 443.5 jit_solution(3888172170574966530)
XLA Ops:
  7.2 0.0 all-gather.2.cloned.1.call-start
  7.2 1.6 pad.13
  8.8 0.0 all-gather.2.cloned.1.call-update
  8.8 5.1 %reshape.108 = bf16[8,16,32,100]{3,2,1,0:T(8,128)(2,1)S(1)} reshape(bf16[4,2,16,3200]{3,2,1,0:T(8,128)(2,1)} %param.6) | data formatting | bytes 1638400 | tf_op jit(solution)/shard_map/reshape | solution.py:659
  13.9 0.3 pad.12
  14.2 3.2 reshape.109.taps_hbm
  17.4 1.1 copy.8
  18.5 0.8 pad.14.cls_ref
  19.3 0.7 convert_multiply_fusion
  19.9 0.7 fusion
  20.7 1.5 select_convert_fusion.oh_hbm
  22.1 77.7 %all-gather.2.cloned.1.call-done.wl_hbm = bf16[3584,768]{1,0:T(8,128)(2,1)} async-done(((bf16[112,768]{1,0:T(8,128)(2,1)}), bf16[3584,768]{1,0:T(8,128)(2,1)}) %all-gather.2.cloned.1.call-update) | async-done | bytes 5505040 | tf_op jit(solution)/shard_map/all_gather | solution.py:662
  99.9 332.7 %shard_map.77 = (f32[216,768]{1,0:T(8,128)}, f32[112,768]{1,0:T(8,128)}) custom-call(bf16[8,16,3584]{2,1,0:T(8,128)(2,1)} %reshape.109.taps_hbm, bf16[3584,768]{1,0:T(8,128)(2,1)} %all-gather.2.cloned.1.call-done.wl_hbm, bf16[9,768,768]{2,1,0:T(8,128)(2,1)} %bitcast.11, bf16[768,256]{1,0:T(8,128)(2,1)} %pad.14.cls_ref, ...), custom_call_target="tpu_custom_call" | custom-call | tf_op jit(solution)/shard_map/pallas_call | solution.py:591
  432.6 1.0 slice_bitcast_fusion
  433.6 1.0 copy.9
  434.6 2.0 copy.11
  (2 shorter events, 0.0 us)
Async XLA Ops:
  7.2 92.7 %all-gather.2.cloned.1.call-start = ((), (), s32[]{:S(2)}) async-start(), calls=%async_computation | async-start | bytes 5677056 | tf_op jit(solution)/shard_map/all_gather | solution.py:662
Sparse Core Ops, SparseCore 0:
  11.2 88.6 all-gather.1

commit v3 on v2

--- a/solution.py
+++ b/solution.py
@@ -16,6 +16,7 @@
 CH = 768
 CK = 256
 NCH = CH // CK
+KROWS = 100
 KPAD = 112
 GROUPS = NX * NZ
 KW = KPAD * GROUPS
@@ -25,6 +26,7 @@
 XC, XL = CROWS * NZ, KPAD * NZ
 UNIT = XC // 9
 HALF = CH // 2
+FARROWS = PIX // 2
 CLASSES = 150
 CPAD = 256
 
@@ -42,11 +44,12 @@
 
 
 def head_kernel(
-    taps_hbm, wl_hbm, w_hbm, cls_ref, oh_hbm, conv_out, lat_out,
-    taps, wl, w, lateral, ext, xin, xout, gin, dsilu, acc, gpv, rim_out, rim_in, oh,
-    ext_all, taps_all, gp_all, gs_all, gpv_all, cols_t, taps_t, part_c, part_l, ring_c, ring_l,
-    local_sem, tap_send, tap_recv, oh_send, oh_recv, x_send, x_recv, halo_send, halo_recv,
-    g_send, g_recv, rim_send, rim_recv, early_sem, e_send, e_recv, a_send, a_recv, rc_send, rc_recv, rl_send, rl_recv,
+    tap_ref, lat_ref, w_hbm, cls_ref, counts_ref, labels_ref, conv_out, lat_out,
+    tap_pad, taps, wl, w, lateral, ext, xin, xout, gin, dsilu, acc, gpv, rim_out, rim_in, oh_own, oh,
+    ext_all, taps_all, transit, gp_all, gs_all, gpv_all, cols_t, taps_t, part_c, part_l, ring_c, ring_l,
+    local_sem, tap_send, tap_recv, pass_send, wz_send, wx_send, wf_send, w_recv, oh_send, oh_recv,
+    x_send, x_recv, halo_send, halo_recv, g_send, g_recv, rim_send, rim_recv,
+    early_sem, t_send, t_recv, a_send, a_recv, rc_send, rc_recv, rl_send, rl_recv,
 ):
     dp = lax.axis_index("dp")
     s = lax.axis_index("section")
@@ -61,20 +64,27 @@
     down = jnp.where(half == 0, pair, dp + NZ)
     src_half = z // 4
     is_first, is_last = s == 0, s == SECTIONS - 1
+    even = s % 2 == 0
+    gx = lateral
+    z_next, z_prev = x * NZ + (z + 1) % NZ, x * NZ + (z + NZ - 1) % NZ
+    x_left, x_right, x_far = (x + NX - 1) % NX, (x + 1) % NX, (x + 2) % NX
+    left, right = x_left * NZ + z, x_right * NZ + z
 
     def home(img):
         return x * NZ + 2 * img + (src_half + odd) % 2
 
-    gx = lateral
-    early = s < 4
-    z_next, z_prev = x * NZ + (z + 1) % NZ, x * NZ + (z + NZ - 1) % NZ
+    def remote(src, dst, send, recv, d, sec):
+        return pltpu.make_async_remote_copy(
+            src_ref=src, dst_ref=dst, send_sem=send, recv_sem=recv,
+            device_id={"dp": d, "section": sec}, device_id_type=MESH,
+        )
+
+    def local_wait(ref, sem):
+        pltpu.make_async_copy(ref, ref, sem).wait()
 
     my_tile = s // 4
     tap_slot = (z % 4) * 4 + s % 4
-
-    wl_copy = pltpu.make_async_copy(wl_hbm, wl, local_sem.at[0])
-    w_copy = pltpu.make_async_copy(w_hbm, w, local_sem.at[1])
-    wl_copy.start()
+    w_copy = pltpu.make_async_copy(w_hbm, w, local_sem.at[0])
     w_copy.start()
 
     barrier = pltpu.get_barrier_semaphore()
@@ -82,20 +92,17 @@
     def greet(d, sec):
         pl.semaphore_signal(barrier, inc=1, device_id={"dp": d, "section": sec}, device_id_type=MESH)
 
-    def tap_source(j):
-        return x * NZ + half * 4 + j // 4, (image % 2) * 4 + j % 4
-
-    for j in range(16):
-        d, sec = tap_source(j)
-
-        @pl.when(jnp.logical_or(d != dp, sec != s))
-        def _():
-            greet(d, sec)
-
-    for k in range(1, NX):
-        greet((x + k) % NX * NZ + z, s)
-    greet(z_next, s)
-    greet(z_prev, s)
+    @pl.when(even)
+    def _():
+        for j in range(16):
+            d, sec = x * NZ + half * 4 + j // 4, (image % 2) * 4 + j % 4
+
+            @pl.when(jnp.logical_or(d != dp, sec != s))
+            def _():
+                greet(d, sec)
+
+    for d in (left, right, z_next, z_prev):
+        greet(d, s)
 
     @pl.when(has_up)
     def _():
@@ -122,12 +129,30 @@
             def _():
                 greet(d, s)
 
+    flat = tap_ref[...].reshape(8 * 16, GROUPS * KROWS).astype(F32)
+    lane = lax.broadcasted_iota(jnp.int32, (8 * 16, 128), 1)
+    for tile in range(KW // 128):
+        first = tile * 128
+        total = jnp.zeros((8 * 16, 128), F32)
+        for g in range(first // KPAD, min((first + 127) // KPAD + 1, GROUPS)):
+            lo = first - (KPAD - KROWS) * g
+            start = min(max(lo // 128 * 128, 0), GROUPS * KROWS - 256)
+            moved = pltpu.roll(flat[:, start:start + 256], (start - lo) % 256, 1)[:, :128]
+            inside = jnp.logical_and(lane + first >= KPAD * g, lane + first < KPAD * g + KROWS)
+            total = jnp.where(inside, moved, total)
+        tap_pad[:, :, first:first + 128] = total.astype(BF16).reshape(8, 16, 128)
+
+    def w_rows(xx, zz):
+        return wl.at[pl.ds(pl.multiple_of((xx * NZ + zz) * KPAD, 16), KPAD), :]
+
+    wl[pl.ds(pl.multiple_of(dp * KPAD, 16), KPAD), :] = lat_ref[...]
+
     def tap_target(k):
-        level, micro, core = k // 4, (k // 2) % 2, k % 2
-        return home(2 * micro + my_tile), 2 * level + core
-
-    need = jnp.int32(NX - 1 + 2)
-    for k in range(16):
+        level, micro = k // 2, k % 2
+        return home(2 * micro + my_tile), 2 * level
+
+    need = jnp.int32(4)
+    for k in range(8):
         d, sec = tap_target(k)
         need += jnp.logical_or(d != dp, sec != s).astype(jnp.int32)
     for flag in (has_up, has_down, s > 0, s < SECTIONS - 1):
@@ -141,16 +166,12 @@
 
     def tap_copy(k):
         d, sec = tap_target(k)
-        return pltpu.make_async_remote_copy(
-            src_ref=taps_hbm.at[k // 2], dst_ref=tap_rows(tap_slot),
-            send_sem=tap_send.at[k], recv_sem=tap_recv.at[tap_slot],
-            device_id={"dp": d, "section": sec}, device_id_type=MESH,
-        )
-
-    def tap_local(k):
-        return pltpu.make_async_copy(taps_hbm.at[k // 2], tap_rows(tap_slot), tap_recv.at[tap_slot])
-
-    for k in range(16):
+        return remote(tap_pad.at[k], tap_rows(tap_slot), tap_send.at[k], tap_recv.at[tap_slot], d, sec)
+
+    def tap_pass(j):
+        return remote(tap_rows(j), tap_rows(j), pass_send.at[j], tap_recv.at[j], dp, s + 1)
+
+    for k in range(8):
         d, sec = tap_target(k)
         other = jnp.logical_or(d != dp, sec != s)
 
@@ -160,23 +181,86 @@
 
         @pl.when(jnp.logical_not(other))
         def _():
-            tap_local(k).start()
+            pltpu.make_async_copy(tap_pad.at[k], tap_rows(tap_slot), tap_recv.at[tap_slot]).start()
+
+    order = (0, -1, 1, -2, 2, -3, 3, -4)
+
+    def ring_z(i):
+        return (z + NZ + order[i]) % NZ
+
+    def w_send_z(i, way):
+        block = w_rows(x, ring_z(i))
+        return remote(
+            block, block, wz_send.at[way, i], w_recv.at[x * NZ + ring_z(i)], z_next if way == 0 else z_prev, s
+        )
+
+    def w_send_x(i, way):
+        block = w_rows(x, ring_z(i))
+        return remote(
+            block, block, wx_send.at[way, i], w_recv.at[x * NZ + ring_z(i)], right if way == 0 else left, s
+        )
+
+    def w_send_far(i):
+        xx = x_left if i % 2 == 0 else x_right
+        block = w_rows(xx, ring_z(i))
+        return remote(
+            block, block, wf_send.at[i], w_recv.at[xx * NZ + ring_z(i)], right if i % 2 == 0 else left, s
+        )
+
+    def w_wait(xx, i):
+        local_wait(w_rows(xx, ring_z(i)), w_recv.at[xx * NZ + ring_z(i)])
+
+    def z_ways(i):
+        ways = []
+        if order[i] <= 0 and order[i] > -4:
+            ways.append(0)
+        if order[i] >= 0 and order[i] < 3:
+            ways.append(1)
+        return ways
+
+    def far_step(i):
+        for xx, forwards in ((x_left, i % 2 == 0), (x_right, i % 2 == 1)):
+            w_wait(xx, i)
+            if forwards:
+                w_send_far(i).start()
+
+    for i in range(NZ):
+        if i > 0:
+            w_wait(x, i)
+        for way in z_ways(i):
+            w_send_z(i, way).start()
+        for way in range(2):
+            w_send_x(i, way).start()
+        if i > 0:
+            far_step(i - 1)
+
+        @pl.when(even)
+        def _():
+            for j in (2 * i, 2 * i + 1):
+                local_wait(tap_rows(j), tap_recv.at[j])
+                tap_pass(j).start()
+
+    far_step(NZ - 1)
 
     def oh_rows(r):
         return oh.at[pl.ds(pl.multiple_of(r * COLS, COLS), COLS), :]
 
     def oh_src(img):
-        return oh_hbm.at[img // 2, pl.ds((img % 2) * COLS, COLS), :]
+        return oh_own.at[img // 2, pl.ds((img % 2) * COLS, COLS), :]
 
     def oh_copy(img):
-        return pltpu.make_async_remote_copy(
-            src_ref=oh_src(img), dst_ref=oh_rows(z % 4),
-            send_sem=oh_send.at[img], recv_sem=oh_recv.at[z % 4],
-            device_id={"dp": home(img), "section": s}, device_id_type=MESH,
-        )
+        return remote(oh_src(img), oh_rows(z % 4), oh_send.at[img], oh_recv.at[z % 4], home(img), s)
 
     @pl.when(is_last)
     def _():
+        sub = lax.broadcasted_iota(jnp.int32, (CPAD, 2 * COLS), 0)
+        tile_of = lax.broadcasted_iota(jnp.int32, (CPAD, 2 * COLS), 1) // COLS
+        for micro in range(2):
+            count = counts_ref[0, micro]
+            share = 1.0 / (count.astype(F32) * (COLS * GROUPS * 2))
+            weight = jnp.where(tile_of < count, share, 0.0)
+            hot = jnp.where(sub == labels_ref[micro:micro + 1, :], 1.0, 0.0)
+            oh_own[micro] = jnp.where(sub == CPAD - 1, weight, hot).T.astype(BF16)
         for img in range(4):
             @pl.when(home(img) != dp)
             def _():
@@ -194,9 +278,13 @@
     def _():
         ext[COLS + PIX:, :] = jnp.zeros((COLS, CH), BF16)
 
-    for j in range(16):
-        pltpu.make_async_copy(tap_rows(j), tap_rows(j), tap_recv.at[j]).wait()
-    wl_copy.wait()
+    @pl.when(jnp.logical_not(even))
+    def _():
+        for j in range(16):
+            local_wait(tap_rows(j), tap_recv.at[j])
+
+    for i in range(NZ):
+        w_wait(x_far, i)
 
     for n in range(NCH):
         lateral[:, n * CK:(n + 1) * CK] = nn(taps[...], wl[:, n * CK:(n + 1) * CK])
@@ -225,9 +313,6 @@
             send_sem=halo_send.at[1, c], recv_sem=halo_recv.at[0, c],
             device_id={"dp": down, "section": s}, device_id_type=MESH,
         )
-
-    def local_wait(ref, sem):
-        pltpu.make_async_copy(ref, ref, sem).wait()
 
     def take_x(c):
         cols = slice(c * CK, (c + 1) * CK)
@@ -314,61 +399,116 @@
 
         dsilu[:, ncols] = sig * (1.0 + pre * (1.0 - sig))
 
-    def early_copies(k):
-        peer = (x + k) % NX
-        to = {"dp": peer * NZ + z, "section": s}
-        at = pl.ds(pl.multiple_of(peer * XL, 128), XL)
+    def gather_copy(buf, kind, way):
+        return remote(
+            buf.at[x], buf.at[x], a_send.at[kind, way], a_recv.at[kind, way], right if way == 0 else left, s
+        )
+
+    def gather_far(buf, kind, way):
+        rows = buf.shape[1] // 2
+        block = buf.at[x_left if way == 0 else x_right, pl.ds(way * rows, rows), :]
+        return remote(
+            block, block, a_send.at[kind, 2 + way], a_recv.at[kind, 2 + way], right if way == 0 else left, s
+        )
+
+    def gather_start(buf, kind):
+        for way in range(2):
+            gather_copy(buf, kind, way).start()
+
+    def gather_forward(buf, kind):
+        for way in range(2):
+            local_wait(buf.at[x_left if way == 0 else x_right], a_recv.at[kind, way])
+            gather_far(buf, kind, way).start()
+
+    def gather_finish(buf, kind):
+        rows = buf.shape[1] // 2
+        for way in range(2):
+            local_wait(buf.at[x_far, pl.ds(way * rows, rows), :], a_recv.at[kind, 2 + way])
+
+    def gather_sent(buf, kind):
+        for way in range(2):
+            gather_copy(buf, kind, way).wait_send()
+            gather_far(buf, kind, way).wait_send()
+
+    def tap_part(xx):
+        return pl.ds(pl.multiple_of(xx * XL, 128), XL)
+
+    def slice_copies(way):
+        to = right if way == 0 else left
+        near = x_right if way == 0 else x_left
         return (
-            pltpu.make_async_remote_copy(
-                src_ref=ext, dst_ref=ext_all.at[x], send_sem=e_send.at[0, k], recv_sem=e_recv.at[0, x],
-                device_id=to, device_id_type=MESH,
+            remote(taps.at[:, tap_part(near)], taps_all.at[x], t_send.at[way], t_recv.at[way], to, s),
+            remote(
+                taps.at[pl.ds(way * FARROWS, FARROWS), tap_part(x_far)], transit.at[way],
+                t_send.at[2 + way], t_recv.at[2 + way], to, s,
             ),
-            pltpu.make_async_remote_copy(
-                src_ref=taps.at[:, at], dst_ref=taps_all.at[x], send_sem=e_send.at[1, k], recv_sem=e_recv.at[1, x],
-                device_id=to, device_id_type=MESH,
-            ),
-        )
-
-    def exchange_early():
-        at = pl.ds(pl.multiple_of(x * XL, 128), XL)
-        pltpu.make_async_copy(ext, ext_all.at[x], e_recv.at[0, x]).start()
-        pltpu.make_async_copy(taps.at[:, at], taps_all.at[x], e_recv.at[1, x]).start()
-        for k in range(1, NX):
-            for copy in early_copies(k):
+        )
+
+    def slice_far(way):
+        source = x_left if way == 0 else x_right
+        return remote(
+            transit.at[way], taps_all.at[source, pl.ds(way * FARROWS, FARROWS), :],
+            t_send.at[4 + way], t_recv.at[4 + way], right if way == 0 else left, s,
+        )
+
+    def early_start():
+        ext_all[x] = ext[...]
+        taps_all[x] = taps[:, tap_part(x)]
+        for way in range(2):
+            for copy in slice_copies(way):
                 copy.start()
-        for src in range(NX):
-            local_wait(ext_all.at[src], e_recv.at[0, src])
-            local_wait(taps_all.at[src], e_recv.at[1, src])
-            lanes_of = slice(src * PIX, (src + 1) * PIX)
-            for dr in range(3):
-                cols_t[dr, :, lanes_of] = ext_all[src, dr * COLS:dr * COLS + PIX, :].T
-            taps_t[:, lanes_of] = taps_all[src].T
-
-    @pl.when(jnp.logical_and(early, s % 2 == 1))
+        gather_start(ext_all, 2)
+
+    def early_forward():
+        for way in range(2):
+            local_wait(transit.at[way], t_recv.at[2 + way])
+            slice_far(way).start()
+        gather_forward(ext_all, 2)
+
+    def turn(src):
+        lanes_of = pl.ds(pl.multiple_of(src * PIX, PIX), PIX)
+        for dr in range(3):
+            cols_t[dr, :, lanes_of] = ext_all[src, dr * COLS:dr * COLS + PIX, :].T
+        taps_t[:, lanes_of] = taps_all[src].T
+
+    def early_finish():
+        for way in range(2):
+            local_wait(taps_all.at[x_left if way == 0 else x_right], t_recv.at[way])
+            local_wait(taps_all.at[x_far, pl.ds(way * FARROWS, FARROWS), :], t_recv.at[4 + way])
+        gather_finish(ext_all, 2)
+
+        @pl.loop(0, NX)
+        def _(src):
+            turn(src)
+
+    @pl.when(jnp.logical_and(s < 6, s % 2 == 1))
     def _():
         pl.semaphore_signal(early_sem, inc=1, device_id={"dp": dp, "section": s - 1}, device_id_type=MESH)
 
-    @pl.when(jnp.logical_and(early, s % 2 == 0))
+    @pl.when(jnp.logical_and(s < 6, s % 2 == 0))
     def _():
         pl.semaphore_wait(early_sem, 1)
 
-    @pl.when(early)
-    def _():
-        exchange_early()
+    @pl.when(s < 6)
+    def _():
+        early_start()
+
+    @pl.when(s < 4)
+    def _():
+        early_forward()
+        early_finish()
 
     @pl.when(is_last)
     def _():
         for r in range(4):
             local_wait(oh_rows(r), oh_recv.at[r])
         logits = nn(xout[...], cls_ref[...])
-        lane = lax.broadcasted_iota(jnp.int32, (PIX, CPAD), 1)
-        real = lane < CLASSES
-        expo = jnp.where(real, jnp.exp(logits), 0.0)
+        spot = lax.broadcasted_iota(jnp.int32, (PIX, CPAD), 1)
+        expo = jnp.exp(logits)
         probs = expo / jnp.sum(expo, axis=-1, keepdims=True)
         marks = oh[...].astype(F32)
-        weight = jnp.sum(jnp.where(lane == CPAD - 1, marks, 0.0), axis=-1, keepdims=True)
-        hot = jnp.where(real, marks, 0.0)
-        grad_logits = ((probs - hot) * weight).astype(BF16)
+        weight = jnp.sum(jnp.where(spot == CPAD - 1, marks, 0.0), axis=-1, keepdims=True)
+        grad_logits = ((probs - marks[:, :CLASSES]) * weight).astype(BF16)
         gx[...] = nt(grad_logits, cls_ref[...])
 
     def g_copy(c):
@@ -462,34 +602,38 @@
         def _():
             g_copy(n).start()
 
-    def ring_copy(kind, k):
-        ref = (gp_all, gs_all)[kind]
-        return pltpu.make_async_remote_copy(
-            src_ref=ref.at[x], dst_ref=ref.at[x], send_sem=a_send.at[kind, k], recv_sem=a_recv.at[kind, x],
-            device_id={"dp": (x + k) % NX * NZ + z, "section": s}, device_id_type=MESH,
-        )
-
-    for kind in range(2):
-        for k in range(1, NX):
-            ring_copy(kind, k).start()
-
-    @pl.when(jnp.logical_not(early))
-    def _():
-        exchange_early()
-
-    def wait_ring(kind, src):
-        @pl.when(src != x)
-        def _():
-            local_wait((gp_all, gs_all)[kind].at[src], a_recv.at[kind, src])
+    gather_start(gp_all, 0)
+    gather_start(gs_all, 1)
+
+    @pl.when(s >= 6)
+    def _():
+        early_start()
+
+    gather_forward(gp_all, 0)
+    gather_forward(gs_all, 1)
+
+    @pl.when(s >= 4)
+    def _():
+        early_forward()
 
     whole_col = lax.broadcasted_iota(jnp.int32, (PIX, CH), 0) % COLS
-    for src in range(NX):
-        wait_ring(0, src)
-        rows = slice(src * PIX, (src + 1) * PIX)
+
+    def spread(src):
+        rows = pl.ds(pl.multiple_of(src * PIX, PIX), PIX)
         value = gp_all[src].astype(F32)
         gpv_all[0, rows, :] = jnp.where(whole_col == COLS - 1, 0.0, pltpu.roll(value, PIX - 1, 0)).astype(BF16)
         gpv_all[1, rows, :] = gp_all[src]
         gpv_all[2, rows, :] = jnp.where(whole_col == 0, 0.0, pltpu.roll(value, 1, 0)).astype(BF16)
+
+    spread(x)
+    spread(x_left)
+    spread(x_right)
+    gather_finish(gp_all, 0)
+    spread(x_far)
+
+    @pl.when(s >= 4)
+    def _():
+        early_finish()
 
     @pl.loop(0, 9)
     def _(u):
@@ -518,11 +662,8 @@
         ring_c[way, 0] = own_rows(part_c, CROWS, way, 0).astype(BF16)
         hop(*conv_ring, way, 0).start()
 
-    for src in range(NX):
-        wait_ring(1, src)
-    spread = gs_all[...].reshape(WIDE, CH)
-
-    part_l[...] = nn(taps_t[...], spread)
+    gather_finish(gs_all, 1)
+    part_l[...] = nn(taps_t[...], gs_all[...].reshape(WIDE, CH))
 
     for way in range(2):
         ring_l[way, 0] = own_rows(part_l, KPAD, way, 0).astype(BF16)
@@ -540,12 +681,24 @@
                 else:
                     out[:, way * HALF:(way + 1) * HALF] = total
 
-    for k in range(16):
+    for k in range(8):
         d, sec = tap_target(k)
 
         @pl.when(jnp.logical_or(d != dp, sec != s))
         def _():
             tap_copy(k).wait_send()
+
+    @pl.when(even)
+    def _():
+        for j in range(16):
+            tap_pass(j).wait_send()
+
+    for i in range(NZ):
+        for way in z_ways(i):
+            w_send_z(i, way).wait_send()
+        for way in range(2):
+            w_send_x(i, way).wait_send()
+        w_send_far(i).wait_send()
 
     @pl.when(is_last)
     def _():
@@ -573,30 +726,33 @@
             halo_down(c).wait_send()
             rim_down(c).wait_send()
 
-    for k in range(1, NX):
-        for copy in early_copies(k):
+    for kind, buf in enumerate((gp_all, gs_all, ext_all)):
+        gather_sent(buf, kind)
+    for way in range(2):
+        for copy in slice_copies(way):
             copy.wait_send()
-        for kind in range(2):
-            ring_copy(kind, k).wait_send()
+        slice_far(way).wait_send()
     for way in range(2):
         for t in range(NZ - 1):
             hop(*conv_ring, way, t).wait_send()
             hop(*lat_ring, way, t).wait_send()
 
 
-def head_call(taps, wl, w, cls, oh):
+def head_call(taps, lat, w, cls, counts, labels):
     dma = pltpu.SemaphoreType.DMA
     hbm = pl.BlockSpec(memory_space=pl.ANY)
     vmem = pl.BlockSpec(memory_space=pltpu.VMEM)
+    smem = pl.BlockSpec(memory_space=pltpu.SMEM)
     return pl.pallas_call(
         head_kernel,
         out_shape=(
             jax.ShapeDtypeStruct((CROWS, CH), F32),
             jax.ShapeDtypeStruct((KPAD, CH), F32),
         ),
-        in_specs=[hbm, hbm, hbm, vmem, hbm],
+        in_specs=[vmem, vmem, hbm, vmem, smem, vmem],
         out_specs=(vmem, vmem),
         scratch_shapes=[
+            pltpu.VMEM((8, 16, KW), BF16),
             pltpu.VMEM((PIX, KW), BF16),
             pltpu.VMEM((KW, CH), BF16),
             pltpu.VMEM((9, CH, CH), BF16),
@@ -610,9 +766,11 @@
             pltpu.VMEM((3, PIX, CH), BF16),
             pltpu.VMEM((2, COLS, CH), BF16),
             pltpu.VMEM((2, COLS, CH), BF16),
+            pltpu.VMEM((2, 2 * COLS, CPAD), BF16),
             pltpu.VMEM((PIX, CPAD), BF16),
             pltpu.VMEM((NX, PIX + 2 * COLS, CH), BF16),
             pltpu.VMEM((NX, PIX, XL), BF16),
+            pltpu.VMEM((2, FARROWS, XL), BF16),
             pltpu.VMEM((NX, PIX, CH), BF16),
             pltpu.VMEM((NX, PIX, CH), BF16),
             pltpu.VMEM((3, WIDE, CH), BF16),
@@ -622,9 +780,14 @@
             pltpu.VMEM((XL, CH), F32),
             pltpu.VMEM((2, NZ, CROWS, HALF), BF16),
             pltpu.VMEM((2, NZ, KPAD, HALF), BF16),
-            dma((2,)),
+            dma((1,)),
+            dma((8,)),
             dma((16,)),
             dma((16,)),
+            dma((2, NZ)),
+            dma((2, NZ)),
+            dma((NZ,)),
+            dma((GROUPS,)),
             dma((4,)),
             dma((4,)),
             dma((NCH,)),
@@ -636,39 +799,29 @@
             dma((2, NCH)),
             dma((2, NCH)),
             pltpu.SemaphoreType.REGULAR,
-            dma((2, NX)),
-            dma((2, NX)),
-            dma((2, NX)),
-            dma((2, NX)),
+            dma((6,)),
+            dma((6,)),
+            dma((3, 4)),
+            dma((3, 4)),
             dma((2, NZ - 1)),
             dma((2, NZ - 1)),
             dma((2, NZ - 1)),
             dma((2, NZ - 1)),
         ],
         compiler_params=pltpu.CompilerParams(
-            collective_id=0, has_side_effects=True, vmem_limit_bytes=60 << 20
+            collective_id=0, has_side_effects=True, vmem_limit_bytes=62 << 20
         ),
-    )(taps, wl, w, cls, oh)
+    )(taps, lat, w, cls, counts, labels)
 
 
 def on_device(tap_maps, lateral_weight, conv_weight, classifier, tile_counts, labels):
     levels, micros, here, width = tap_maps.shape
-    per = width // GROUPS
-    classes = classifier.shape[1]
-    pixels = labels.shape[1]
-    grouped = tap_maps.reshape(levels * micros, here, GROUPS, per)
-    taps = jnp.pad(grouped, ((0, 0), (0, 0), (0, 0), (0, KPAD - per))).reshape(levels * micros, here, KW)
-    own = jnp.pad(lateral_weight[0], ((0, KPAD - per), (0, 0)))
-    wl = lax.all_gather(own, "dp", axis=0, tiled=True)
-    cls = jnp.pad(classifier, ((0, 0), (0, CPAD - classes)))
-    counts = tile_counts[0][:, None]
-    valid = (jnp.arange(pixels)[None, :] // COLS < counts).astype(F32)
-    weight = valid / (counts.astype(F32) * COLS * GROUPS * micros)
-    lane = jnp.arange(CPAD)
-    hot = (labels[:, :, None] == lane).astype(F32)
-    oh = jnp.where(lane == CPAD - 1, weight[:, :, None], hot).astype(BF16)
-    conv_grad, lateral_grad = head_call(taps, wl, conv_weight.reshape(9, CH, CH), cls, oh)
-    return (conv_grad[None], lateral_grad[None, :per])
+    taps = tap_maps.reshape(levels * micros, here, width)
+    lat = jnp.pad(lateral_weight[0], ((0, KPAD - KROWS), (0, 0)))
+    conv_grad, lateral_grad = head_call(
+        taps, lat, conv_weight.reshape(9, CH, CH), classifier, tile_counts, labels
+    )
+    return (conv_grad[None], lateral_grad[None, :KROWS])
 
 
 def solution(mesh):

time: 444 us -> 317 us (0.71)
  the two profiles are of different devices: /device:TPU:16 before, /device:TPU:2 now
where the time goes in v3:
time: 317 us; the launch traced here: 316 us
  Pallas kernels  308 us (97%)
  local copies, waits for them, and re-layouts  7.45 us (2%)
    pallas_call x1, Pallas kernels, head_call(): pl.pallas_call(head_kernel, out_shape=(jax.ShapeDtypeStruct((CROWS, CH),...  308 us

profile of v3, /device:TPU:2, one launch (start us, length us, event | category | flops | bytes accessed | tf_op | source)
XLA Modules:
  0.0 316.4 jit_solution(11998714674841067242)
XLA Ops:
  0.6 1.6 pad.4.lat_ref
  2.2 1.9 copy.8.cls_ref
  4.1 308.3 %shard_map.77 = (f32[216,768]{1,0:T(8,128)}, f32[112,768]{1,0:T(8,128)}) custom-call(bf16[8,16,3200]{2,1,0:T(8,128)(2,1)} %bitcast.7, bf16[112,768]{1,0:T(8,128)(2,1)} %pad.4.lat_ref, bf16[9,768,768]{2,1,0:T(8,128)(2,1)} %bitcast.6, bf16[768,150]{1,0:T(8,128)(2,1)} %copy.8.cls_ref, s32[1,2]{1,0:T(1,128)} %counts_ref.1, s32[2,128]{1,0:T(2,128)} %labels_ref.1), custom_call_target="tpu_custom_call" | custom-call | tf_op jit(solution)/shard_map/pallas_call | solution.py:746
  312.4 1.0 slice_bitcast_fusion
  313.4 1.0 copy.9
  314.4 2.0 copy.11

commit v4 on v3

--- a/solution.py
+++ b/solution.py
@@ -45,11 +45,13 @@
 
 def head_kernel(
     tap_ref, lat_ref, w_hbm, cls_ref, counts_ref, labels_ref, conv_out, lat_out,
-    tap_pad, taps, wl, w, lateral, ext, xin, xout, gin, dsilu, acc, gpv, rim_out, rim_in, oh_own, oh,
-    ext_all, taps_all, transit, gp_all, gs_all, gpv_all, cols_t, taps_t, part_c, part_l, ring_c, ring_l,
-    local_sem, tap_send, tap_recv, pass_send, wz_send, wx_send, wf_send, w_recv, oh_send, oh_recv,
+    tap_pad, wl, w, gx, lat_send, lat_far, lat_near, lat_nat, lat_img,
+    ext, xin, xout, gin, dsilu, acc, gpv, rim_out, rim_in, oh_own, oh,
+    ext_all, taps_all, gs_img, gp_all, gs_all, gpv_all, cols_t, taps_t, part_c, part_l, ring_c, ring_l,
+    local_sem, tap_send, tap_recv, pass_send, pass_recv, wz_send, w_recv,
+    lf_send, lf_recv, ln_send, ln_recv, lz_send, lz_recv, oh_send, oh_recv,
     x_send, x_recv, halo_send, halo_recv, g_send, g_recv, rim_send, rim_recv,
-    early_sem, t_send, t_recv, a_send, a_recv, rc_send, rc_recv, rl_send, rl_recv,
+    early_sem, gz_send, gz_recv, a_send, a_recv, rc_send, rc_recv, rl_send, rl_recv,
 ):
     dp = lax.axis_index("dp")
     s = lax.axis_index("section")
@@ -65,7 +67,6 @@
     src_half = z // 4
     is_first, is_last = s == 0, s == SECTIONS - 1
     even = s % 2 == 0
-    gx = lateral
     z_next, z_prev = x * NZ + (z + 1) % NZ, x * NZ + (z + NZ - 1) % NZ
     x_left, x_right, x_far = (x + NX - 1) % NX, (x + 1) % NX, (x + 2) % NX
     left, right = x_left * NZ + z, x_right * NZ + z
@@ -82,8 +83,6 @@
     def local_wait(ref, sem):
         pltpu.make_async_copy(ref, ref, sem).wait()
 
-    my_tile = s // 4
-    tap_slot = (z % 4) * 4 + s % 4
     w_copy = pltpu.make_async_copy(w_hbm, w, local_sem.at[0])
     w_copy.start()
 
@@ -94,12 +93,11 @@
 
     @pl.when(even)
     def _():
-        for j in range(16):
-            d, sec = x * NZ + half * 4 + j // 4, (image % 2) * 4 + j % 4
-
-            @pl.when(jnp.logical_or(d != dp, sec != s))
-            def _():
-                greet(d, sec)
+        for xx in range(NX):
+            for sec in range(SECTIONS):
+                @pl.when(jnp.logical_or(xx != x, sec != s))
+                def _():
+                    greet(xx * NZ + z, sec)
 
     for d in (left, right, z_next, z_prev):
         greet(d, s)
@@ -120,11 +118,11 @@
     def _():
         greet(dp, s + 1)
 
-    @pl.when(is_last)
-    def _():
-        for j in range(4):
-            d = x * NZ + half * 4 + j
-
+    def native(r):
+        return x * NZ + half * 4 + r
+
+    for r in range(4):
+        for d in (native(r), home(r)):
             @pl.when(d != dp)
             def _():
                 greet(d, s)
@@ -142,46 +140,46 @@
             total = jnp.where(inside, moved, total)
         tap_pad[:, :, first:first + 128] = total.astype(BF16).reshape(8, 16, 128)
 
-    def w_rows(xx, zz):
-        return wl.at[pl.ds(pl.multiple_of((xx * NZ + zz) * KPAD, 16), KPAD), :]
-
-    wl[pl.ds(pl.multiple_of(dp * KPAD, 16), KPAD), :] = lat_ref[...]
-
-    def tap_target(k):
-        level, micro = k // 2, k % 2
-        return home(2 * micro + my_tile), 2 * level
-
-    need = jnp.int32(4)
-    for k in range(8):
-        d, sec = tap_target(k)
-        need += jnp.logical_or(d != dp, sec != s).astype(jnp.int32)
+    def w_rows(zz):
+        return wl.at[pl.ds(pl.multiple_of(zz * KPAD, 16), KPAD), :]
+
+    wl[pl.ds(pl.multiple_of(z * KPAD, 16), KPAD), :] = lat_ref[...]
+
+    need = jnp.where(even, 4 + 15, 4 + 16)
     for flag in (has_up, has_down, s > 0, s < SECTIONS - 1):
         need += flag.astype(jnp.int32)
-    for img in range(4):
-        need += jnp.logical_and(is_last, home(img) != dp).astype(jnp.int32)
+    for r in range(4):
+        need += (native(r) != dp).astype(jnp.int32) + (home(r) != dp).astype(jnp.int32)
     pl.semaphore_wait(barrier, need)
 
-    def tap_rows(j):
-        return taps.at[pl.ds(pl.multiple_of((j // 4) * COLS + (j % 4) * 16, 16), 16), :]
-
-    def tap_copy(k):
-        d, sec = tap_target(k)
-        return remote(tap_pad.at[k], tap_rows(tap_slot), tap_send.at[k], tap_recv.at[tap_slot], d, sec)
-
-    def tap_pass(j):
-        return remote(tap_rows(j), tap_rows(j), pass_send.at[j], tap_recv.at[j], dp, s + 1)
+    def tap_cell(xx, j):
+        return taps_all.at[xx, pl.ds(pl.multiple_of(j * 16, 16), 16), :]
+
+    def tap_src(k, xx):
+        return tap_pad.at[k, :, pl.ds(xx * XL, XL)]
+
+    def tap_copy(k, xx):
+        slot = (k % 2) * SECTIONS + s
+        return remote(
+            tap_src(k, xx), tap_cell(x, slot), tap_send.at[k, xx], tap_recv.at[x, slot], xx * NZ + z, k // 2 * 2
+        )
+
+    def tap_pass(xx):
+        return remote(taps_all.at[xx], taps_all.at[xx], pass_send.at[xx], pass_recv.at[xx], dp, s + 1)
+
+    def elsewhere(k, xx):
+        return jnp.logical_or(xx != x, k // 2 * 2 != s)
 
     for k in range(8):
-        d, sec = tap_target(k)
-        other = jnp.logical_or(d != dp, sec != s)
-
-        @pl.when(other)
-        def _():
-            tap_copy(k).start()
-
-        @pl.when(jnp.logical_not(other))
-        def _():
-            pltpu.make_async_copy(tap_pad.at[k], tap_rows(tap_slot), tap_recv.at[tap_slot]).start()
+        for xx in range(NX):
+            @pl.when(elsewhere(k, xx))
+            def _():
+                tap_copy(k, xx).start()
+
+            @pl.when(jnp.logical_not(elsewhere(k, xx)))
+            def _():
+                slot = (k % 2) * SECTIONS + s
+                pltpu.make_async_copy(tap_src(k, xx), tap_cell(x, slot), tap_recv.at[x, slot]).start()
 
     order = (0, -1, 1, -2, 2, -3, 3, -4)
 
@@ -189,26 +187,8 @@
         return (z + NZ + order[i]) % NZ
 
     def w_send_z(i, way):
-        block = w_rows(x, ring_z(i))
-        return remote(
-            block, block, wz_send.at[way, i], w_recv.at[x * NZ + ring_z(i)], z_next if way == 0 else z_prev, s
-        )
-
-    def w_send_x(i, way):
-        block = w_rows(x, ring_z(i))
-        return remote(
-            block, block, wx_send.at[way, i], w_recv.at[x * NZ + ring_z(i)], right if way == 0 else left, s
-        )
-
-    def w_send_far(i):
-        xx = x_left if i % 2 == 0 else x_right
-        block = w_rows(xx, ring_z(i))
-        return remote(
-            block, block, wf_send.at[i], w_recv.at[xx * NZ + ring_z(i)], right if i % 2 == 0 else left, s
-        )
-
-    def w_wait(xx, i):
-        local_wait(w_rows(xx, ring_z(i)), w_recv.at[xx * NZ + ring_z(i)])
+        block = w_rows(ring_z(i))
+        return remote(block, block, wz_send.at[way, i], w_recv.at[ring_z(i)], z_next if way == 0 else z_prev, s)
 
     def z_ways(i):
         ways = []
@@ -218,29 +198,11 @@
             ways.append(1)
         return ways
 
-    def far_step(i):
-        for xx, forwards in ((x_left, i % 2 == 0), (x_right, i % 2 == 1)):
-            w_wait(xx, i)
-            if forwards:
-                w_send_far(i).start()
-
     for i in range(NZ):
         if i > 0:
-            w_wait(x, i)
+            local_wait(w_rows(ring_z(i)), w_recv.at[ring_z(i)])
         for way in z_ways(i):
             w_send_z(i, way).start()
-        for way in range(2):
-            w_send_x(i, way).start()
-        if i > 0:
-            far_step(i - 1)
-
-        @pl.when(even)
-        def _():
-            for j in (2 * i, 2 * i + 1):
-                local_wait(tap_rows(j), tap_recv.at[j])
-                tap_pass(j).start()
-
-    far_step(NZ - 1)
 
     def oh_rows(r):
         return oh.at[pl.ds(pl.multiple_of(r * COLS, COLS), COLS), :]
@@ -278,16 +240,72 @@
     def _():
         ext[COLS + PIX:, :] = jnp.zeros((COLS, CH), BF16)
 
+    @pl.when(even)
+    def _():
+        for xx in range(NX):
+            for j in range(2 * SECTIONS):
+                local_wait(tap_cell(xx, j), tap_recv.at[xx, j])
+            tap_pass(xx).start()
+
     @pl.when(jnp.logical_not(even))
     def _():
-        for j in range(16):
-            local_wait(tap_rows(j), tap_recv.at[j])
-
-    for i in range(NZ):
-        w_wait(x_far, i)
-
-    for n in range(NCH):
-        lateral[:, n * CK:(n + 1) * CK] = nn(taps[...], wl[:, n * CK:(n + 1) * CK])
+        for xx in range(NX):
+            local_wait(taps_all.at[xx], pass_recv.at[xx])
+
+    first_rows, last_rows = pl.ds(0, FARROWS), pl.ds(FARROWS, FARROWS)
+    half_rows = (first_rows, last_rows)
+
+    def far_copy(way):
+        return remote(
+            lat_send.at[2, half_rows[way]], lat_far.at[way], lf_send.at[way], lf_recv.at[way],
+            right if way == 0 else left, s,
+        )
+
+    def near_copy(way, part):
+        return remote(
+            lat_send.at[way, half_rows[part]], lat_near.at[way, half_rows[part]],
+            ln_send.at[way, part], ln_recv.at[way, part], right if way == 0 else left, s,
+        )
+
+    lat_send[2] = nn(taps_all[x_far], wl[...]).astype(BF16)
+    for way in range(2):
+        far_copy(way).start()
+    for way in range(2):
+        acc[way] = nn(taps_all[x_right if way == 0 else x_left], wl[...])
+        rows = half_rows[1 - way]
+        lat_send[way, rows] = acc[way, rows].astype(BF16)
+        near_copy(way, 1 - way).start()
+    acc[2] = nn(taps_all[x], wl[...])
+    for way in range(2):
+        rows = half_rows[way]
+        local_wait(lat_far.at[way], lf_recv.at[way])
+        lat_send[way, rows] = (acc[way, rows] + lat_far[way].astype(F32)).astype(BF16)
+        near_copy(way, way).start()
+    for part in range(2):
+        rows = half_rows[part]
+        for way in (1 - part, part):
+            local_wait(lat_near.at[way, rows], ln_recv.at[way, part])
+        lat_nat[rows] = (
+            acc[2, rows] + lat_near[0, rows].astype(F32) + lat_near[1, rows].astype(F32)
+        ).astype(BF16)
+
+    def band(ref, j):
+        return ref.at[pl.ds(pl.multiple_of(j * COLS, COLS), COLS), :]
+
+    def lat_copy(img):
+        return remote(band(lat_nat, img), band(lat_img, z % 4), lz_send.at[img], lz_recv.at[z % 4], home(img), s)
+
+    for img in range(4):
+        @pl.when(home(img) != dp)
+        def _():
+            lat_copy(img).start()
+
+        @pl.when(home(img) == dp)
+        def _():
+            pltpu.make_async_copy(band(lat_nat, img), band(lat_img, z % 4), lz_recv.at[z % 4]).start()
+
+    for r in range(4):
+        local_wait(band(lat_img, r), lz_recv.at[r])
     w_copy.wait()
 
     def lanes(c):
@@ -319,12 +337,12 @@
 
         @pl.when(is_first)
         def _():
-            ext[COLS:COLS + PIX, cols] = lateral[:, cols].astype(BF16)
+            ext[COLS:COLS + PIX, cols] = lat_img[:, cols]
 
         @pl.when(s > 0)
         def _():
             local_wait(xin.at[:, lanes(c)], x_recv.at[c])
-            ext[COLS:COLS + PIX, cols] = (xin[:, cols].astype(F32) + lateral[:, cols]).astype(BF16)
+            ext[COLS:COLS + PIX, cols] = (xin[:, cols].astype(F32) + lat_img[:, cols].astype(F32)).astype(BF16)
 
         @pl.when(has_up)
         def _():
@@ -430,56 +448,19 @@
             gather_copy(buf, kind, way).wait_send()
             gather_far(buf, kind, way).wait_send()
 
-    def tap_part(xx):
-        return pl.ds(pl.multiple_of(xx * XL, 128), XL)
-
-    def slice_copies(way):
-        to = right if way == 0 else left
-        near = x_right if way == 0 else x_left
-        return (
-            remote(taps.at[:, tap_part(near)], taps_all.at[x], t_send.at[way], t_recv.at[way], to, s),
-            remote(
-                taps.at[pl.ds(way * FARROWS, FARROWS), tap_part(x_far)], transit.at[way],
-                t_send.at[2 + way], t_recv.at[2 + way], to, s,
-            ),
-        )
-
-    def slice_far(way):
-        source = x_left if way == 0 else x_right
-        return remote(
-            transit.at[way], taps_all.at[source, pl.ds(way * FARROWS, FARROWS), :],
-            t_send.at[4 + way], t_recv.at[4 + way], right if way == 0 else left, s,
-        )
-
     def early_start():
         ext_all[x] = ext[...]
-        taps_all[x] = taps[:, tap_part(x)]
-        for way in range(2):
-            for copy in slice_copies(way):
-                copy.start()
         gather_start(ext_all, 2)
 
-    def early_forward():
-        for way in range(2):
-            local_wait(transit.at[way], t_recv.at[2 + way])
-            slice_far(way).start()
-        gather_forward(ext_all, 2)
-
-    def turn(src):
-        lanes_of = pl.ds(pl.multiple_of(src * PIX, PIX), PIX)
-        for dr in range(3):
-            cols_t[dr, :, lanes_of] = ext_all[src, dr * COLS:dr * COLS + PIX, :].T
-        taps_t[:, lanes_of] = taps_all[src].T
-
     def early_finish():
-        for way in range(2):
-            local_wait(taps_all.at[x_left if way == 0 else x_right], t_recv.at[way])
-            local_wait(taps_all.at[x_far, pl.ds(way * FARROWS, FARROWS), :], t_recv.at[4 + way])
         gather_finish(ext_all, 2)
 
         @pl.loop(0, NX)
         def _(src):
-            turn(src)
+            lanes_of = pl.ds(pl.multiple_of(src * PIX, PIX), PIX)
+            for dr in range(3):
+                cols_t[dr, :, lanes_of] = ext_all[src, dr * COLS:dr * COLS + PIX, :].T
+            taps_t[:, lanes_of] = taps_all[src].T
 
     @pl.when(jnp.logical_and(s < 6, s % 2 == 1))
     def _():
@@ -495,7 +476,7 @@
 
     @pl.when(s < 4)
     def _():
-        early_forward()
+        gather_forward(ext_all, 2)
         early_finish()
 
     @pl.when(is_last)
@@ -513,7 +494,7 @@
 
     def g_copy(c):
         return pltpu.make_async_remote_copy(
-            src_ref=gs_all.at[x, :, lanes(c)], dst_ref=gin.at[:, lanes(c)],
+            src_ref=gs_img.at[:, lanes(c)], dst_ref=gin.at[:, lanes(c)],
             send_sem=g_send.at[c], recv_sem=g_recv.at[c],
             device_id={"dp": dp, "section": s - 1}, device_id_type=MESH,
         )
@@ -596,25 +577,40 @@
             local_wait(rim_in.at[1, :, lanes(n)], rim_recv.at[1, n])
             acc[1, PIX - COLS:, ncols] += rim_in[1, :, ncols].astype(F32)
 
-        gs_all[x, :, ncols] = acc[1, :, ncols].astype(BF16)
+        gs_img[:, ncols] = acc[1, :, ncols].astype(BF16)
 
         @pl.when(s > 0)
         def _():
             g_copy(n).start()
 
+    def gz_copy(r):
+        return remote(
+            band(gs_img, r), band(gs_all.at[x], image), gz_send.at[r], gz_recv.at[image], native(r), s
+        )
+
+    for r in range(4):
+        @pl.when(native(r) != dp)
+        def _():
+            gz_copy(r).start()
+
+        @pl.when(native(r) == dp)
+        def _():
+            pltpu.make_async_copy(band(gs_img, r), band(gs_all.at[x], image), gz_recv.at[image]).start()
+
     gather_start(gp_all, 0)
+
+    @pl.when(s >= 6)
+    def _():
+        early_start()
+
+    gather_forward(gp_all, 0)
+    for img in range(4):
+        local_wait(band(gs_all.at[x], img), gz_recv.at[img])
     gather_start(gs_all, 1)
 
-    @pl.when(s >= 6)
-    def _():
-        early_start()
-
-    gather_forward(gp_all, 0)
-    gather_forward(gs_all, 1)
-
     @pl.when(s >= 4)
     def _():
-        early_forward()
+        gather_forward(ext_all, 2)
 
     whole_col = lax.broadcasted_iota(jnp.int32, (PIX, CH), 0) % COLS
 
@@ -628,6 +624,7 @@
     spread(x)
     spread(x_left)
     spread(x_right)
+    gather_forward(gs_all, 1)
     gather_finish(gp_all, 0)
     spread(x_far)
 
@@ -682,23 +679,27 @@
                     out[:, way * HALF:(way + 1) * HALF] = total
 
     for k in range(8):
-        d, sec = tap_target(k)
-
-        @pl.when(jnp.logical_or(d != dp, sec != s))
-        def _():
-            tap_copy(k).wait_send()
+        for xx in range(NX):
+            @pl.when(elsewhere(k, xx))
+            def _():
+                tap_copy(k, xx).wait_send()
 
     @pl.when(even)
     def _():
-        for j in range(16):
-            tap_pass(j).wait_send()
+        for xx in range(NX):
+            tap_pass(xx).wait_send()
 
     for i in range(NZ):
         for way in z_ways(i):
             w_send_z(i, way).wait_send()
-        for way in range(2):
-            w_send_x(i, way).wait_send()
-        w_send_far(i).wait_send()
+    for way in range(2):
+        far_copy(way).wait_send()
+        for part in range(2):
+            near_copy(way, part).wait_send()
+    for r in range(4):
+        @pl.when(home(r) != dp)
+        def _():
+            lat_copy(r).wait_send()
 
     @pl.when(is_last)
     def _():
@@ -728,10 +729,11 @@
 
     for kind, buf in enumerate((gp_all, gs_all, ext_all)):
         gather_sent(buf, kind)
-    for way in range(2):
-        for copy in slice_copies(way):
-            copy.wait_send()
-        slice_far(way).wait_send()
+    for r in range(4):
+        @pl.when(native(r) != dp)
+        def _():
+            gz_copy(r).wait_send()
+
     for way in range(2):
         for t in range(NZ - 1):
             hop(*conv_ring, way, t).wait_send()
@@ -753,10 +755,14 @@
         out_specs=(vmem, vmem),
         scratch_shapes=[
             pltpu.VMEM((8, 16, KW), BF16),
-            pltpu.VMEM((PIX, KW), BF16),
-            pltpu.VMEM((KW, CH), BF16),
+            pltpu.VMEM((XL, CH), BF16),
             pltpu.VMEM((9, CH, CH), BF16),
             pltpu.VMEM((PIX, CH), F32),
+            pltpu.VMEM((3, PIX, CH), BF16),
+            pltpu.VMEM((2, FARROWS, CH), BF16),
+            pltpu.VMEM((2, PIX, CH), BF16),
+            pltpu.VMEM((PIX, CH), BF16),
+            pltpu.VMEM((PIX, CH), BF16),
             pltpu.VMEM((PIX + 2 * COLS, CH), BF16),
             pltpu.VMEM((PIX, CH), BF16),
             pltpu.VMEM((PIX, CH), BF16),
@@ -770,7 +776,7 @@
             pltpu.VMEM((PIX, CPAD), BF16),
             pltpu.VMEM((NX, PIX + 2 * COLS, CH), BF16),
             pltpu.VMEM((NX, PIX, XL), BF16),
-            pltpu.VMEM((2, FARROWS, XL), BF16),
+            pltpu.VMEM((PIX, CH), BF16),
             pltpu.VMEM((NX, PIX, CH), BF16),
             pltpu.VMEM((NX, PIX, CH), BF16),
             pltpu.VMEM((3, WIDE, CH), BF16),
@@ -781,13 +787,18 @@
             pltpu.VMEM((2, NZ, CROWS, HALF), BF16),
             pltpu.VMEM((2, NZ, KPAD, HALF), BF16),
             dma((1,)),
-            dma((8,)),
-            dma((16,)),
-            dma((16,)),
-            dma((2, NZ)),
+            dma((8, NX)),
+            dma((NX, 2 * SECTIONS)),
+            dma((NX,)),
+            dma((NX,)),
             dma((2, NZ)),
             dma((NZ,)),
-            dma((GROUPS,)),
+            dma((2,)),
+            dma((2,)),
+            dma((2, 2)),
+            dma((2, 2)),
+            dma((4,)),
+            dma((4,)),
             dma((4,)),
             dma((4,)),
             dma((NCH,)),
@@ -799,8 +810,8 @@
             dma((2, NCH)),
             dma((2, NCH)),
             pltpu.SemaphoreType.REGULAR,
-            dma((6,)),
-            dma((6,)),
+            dma((4,)),
+            dma((4,)),
             dma((3, 4)),
             dma((3, 4)),
             dma((2, NZ - 1)),

time: 317 us -> 275 us (0.87)
  Pallas kernels: 308 us -> 267 us
    pallas_call x1, Pallas kernels: 308 us -> 267 us  [head_call(): pl.pallas_call(head_kernel, out_shape=(jax.ShapeDtypeStruct((CROWS, CH),...]
where the time goes in v4:
time: 275 us
  Pallas kernels  267 us (97%)
  local copies, waits for them, and re-layouts  7.45 us (3%)
    pallas_call x1, Pallas kernels, head_call(): pl.pallas_call(head_kernel, out_shape=(jax.ShapeDtypeStruct((CROWS, CH),...  267 us

profile of v4, /device:TPU:2, one launch (start us, length us, event | category | flops | bytes accessed | tf_op | source)
XLA Modules:
  0.0 275.0 jit_solution(3838517095342035494)
XLA Ops:
  0.6 1.6 pad.4.lat_ref
  2.2 1.9 copy.8.cls_ref
  4.1 266.9 %shard_map.77 = (f32[216,768]{1,0:T(8,128)}, f32[112,768]{1,0:T(8,128)}) custom-call(bf16[8,16,3200]{2,1,0:T(8,128)(2,1)} %bitcast.7, bf16[112,768]{1,0:T(8,128)(2,1)} %pad.4.lat_ref, bf16[9,768,768]{2,1,0:T(8,128)(2,1)} %bitcast.6, bf16[768,150]{1,0:T(8,128)(2,1)} %copy.8.cls_ref, s32[1,2]{1,0:T(1,128)} %counts_ref.1, s32[2,128]{1,0:T(2,128)} %labels_ref.1), custom_call_target="tpu_custom_call" | custom-call | tf_op jit(solution)/shard_map/pallas_call | solution.py:748
  271.0 1.0 slice_bitcast_fusion
  272.0 1.0 copy.9
  273.0 2.0 copy.11

commit v5 on v4

--- a/solution.py
+++ b/solution.py
@@ -47,10 +47,12 @@
     tap_ref, lat_ref, w_hbm, cls_ref, counts_ref, labels_ref, conv_out, lat_out,
     tap_pad, wl, w, gx, lat_send, lat_far, lat_near, lat_nat, lat_img,
     ext, xin, xout, gin, dsilu, acc, gpv, rim_out, rim_in, oh_own, oh,
+    lat_halo, x_halo, g_out, g_rim,
     ext_all, taps_all, gs_img, gp_all, gs_all, gpv_all, cols_t, taps_t, part_c, part_l, ring_c, ring_l,
     local_sem, tap_send, tap_recv, pass_send, pass_recv, wz_send, w_recv,
     lf_send, lf_recv, ln_send, ln_recv, lz_send, lz_recv, oh_send, oh_recv,
     x_send, x_recv, halo_send, halo_recv, g_send, g_recv, rim_send, rim_recv,
+    lh_send, lh_recv, xh_send, xh_recv, gr_send, gr_recv,
     early_sem, gz_send, gz_recv, a_send, a_recv, rc_send, rc_recv, rl_send, rl_recv,
 ):
     dp = lax.axis_index("dp")
@@ -67,6 +69,7 @@
     src_half = z // 4
     is_first, is_last = s == 0, s == SECTIONS - 1
     even = s % 2 == 0
+    sibling = s + 1 - 2 * (s % 2)
     z_next, z_prev = x * NZ + (z + 1) % NZ, x * NZ + (z + NZ - 1) % NZ
     x_left, x_right, x_far = (x + NX - 1) % NX, (x + 1) % NX, (x + 2) % NX
     left, right = x_left * NZ + z, x_right * NZ + z
@@ -105,10 +108,12 @@
     @pl.when(has_up)
     def _():
         greet(up, s)
+        greet(up, sibling)
 
     @pl.when(has_down)
     def _():
         greet(down, s)
+        greet(down, sibling)
 
     @pl.when(s > 0)
     def _():
@@ -146,7 +151,7 @@
     wl[pl.ds(pl.multiple_of(z * KPAD, 16), KPAD), :] = lat_ref[...]
 
     need = jnp.where(even, 4 + 15, 4 + 16)
-    for flag in (has_up, has_down, s > 0, s < SECTIONS - 1):
+    for flag in (has_up, has_down, has_up, has_down, s > 0, s < SECTIONS - 1):
         need += flag.astype(jnp.int32)
     for r in range(4):
         need += (native(r) != dp).astype(jnp.int32) + (home(r) != dp).astype(jnp.int32)
@@ -306,6 +311,21 @@
 
     for r in range(4):
         local_wait(band(lat_img, r), lz_recv.at[r])
+
+    def lat_up():
+        return remote(band(lat_img, 0), lat_halo.at[1], lh_send.at[0], lh_recv.at[1], up, s)
+
+    def lat_down():
+        return remote(band(lat_img, ROWS - 1), lat_halo.at[0], lh_send.at[1], lh_recv.at[0], down, s)
+
+    @pl.when(jnp.logical_and(has_up, jnp.logical_not(even)))
+    def _():
+        lat_up().start()
+
+    @pl.when(jnp.logical_and(has_down, jnp.logical_not(even)))
+    def _():
+        lat_down().start()
+
     w_copy.wait()
 
     def lanes(c):
@@ -332,6 +352,28 @@
             device_id={"dp": down, "section": s}, device_id_type=MESH,
         )
 
+    def edge_up(c):
+        return remote(
+            xout.at[pl.ds(0, COLS), lanes(c)], x_halo.at[1, :, lanes(c)],
+            xh_send.at[0, c], xh_recv.at[1, c], up, s + 1,
+        )
+
+    def edge_down(c):
+        return remote(
+            xout.at[pl.ds(PIX - COLS, COLS), lanes(c)], x_halo.at[0, :, lanes(c)],
+            xh_send.at[1, c], xh_recv.at[0, c], down, s + 1,
+        )
+
+    def take_edges(c):
+        cols = slice(c * CK, (c + 1) * CK)
+        for side, flag, rows in ((0, has_up, slice(0, COLS)), (1, has_down, slice(COLS + PIX, 2 * COLS + PIX))):
+            @pl.when(flag)
+            def _():
+                local_wait(x_halo.at[side, :, lanes(c)], xh_recv.at[side, c])
+                ext[rows, cols] = (
+                    x_halo[side, :, cols].astype(F32) + lat_halo[side, :, cols].astype(F32)
+                ).astype(BF16)
+
     def take_x(c):
         cols = slice(c * CK, (c + 1) * CK)
 
@@ -344,11 +386,11 @@
             local_wait(xin.at[:, lanes(c)], x_recv.at[c])
             ext[COLS:COLS + PIX, cols] = (xin[:, cols].astype(F32) + lat_img[:, cols].astype(F32)).astype(BF16)
 
-        @pl.when(has_up)
+        @pl.when(jnp.logical_and(has_up, even))
         def _():
             halo_up(c).start()
 
-        @pl.when(has_down)
+        @pl.when(jnp.logical_and(has_down, even))
         def _():
             halo_down(c).start()
 
@@ -390,23 +432,14 @@
     def after(v):
         return jnp.where(col == COLS - 1, 0.0, pltpu.roll(v, PIX - 1, 0))
 
-    take_x(0)
-    take_x(1)
-    conv_inner(0, True)
-    wait_halo(0)
-    conv_outer(0)
-    take_x(2)
-    conv_inner(1, False)
-    conv_inner(2, False)
-    wait_halo(1)
-    conv_outer(1)
-    wait_halo(2)
-    for n in range(NCH):
+    def conv_finish(n, chunks, direct):
         ncols = slice(n * CK, (n + 1) * CK)
-        parts = [
-            acc[dc + 1, :, ncols] + conv_part(2, -1, dc, ncols) + conv_part(2, 1, dc, ncols)
-            for dc in (-1, 0, 1)
-        ]
+        parts = []
+        for dc in (-1, 0, 1):
+            part = acc[dc + 1, :, ncols]
+            for c in chunks:
+                part += conv_part(c, -1, dc, ncols) + conv_part(c, 1, dc, ncols)
+            parts.append(part)
         pre = before(parts[0]) + parts[1] + after(parts[2])
         sig = 1.0 / (1.0 + jnp.exp(-pre))
         xout[:, ncols] = (pre * sig).astype(BF16)
@@ -415,7 +448,52 @@
         def _():
             x_copy(n).start()
 
+        if direct:
+            @pl.when(has_up)
+            def _():
+                edge_up(n).start()
+
+            @pl.when(has_down)
+            def _():
+                edge_down(n).start()
+
         dsilu[:, ncols] = sig * (1.0 + pre * (1.0 - sig))
+
+    @pl.when(even)
+    def _():
+        take_x(0)
+        conv_inner(0, True)
+        take_x(1)
+        conv_inner(1, False)
+        wait_halo(0)
+        conv_outer(0)
+        take_x(2)
+        conv_inner(2, False)
+        wait_halo(1)
+        conv_outer(1)
+        wait_halo(2)
+        for n in range(NCH):
+            conv_finish(n, (2,), True)
+
+    @pl.when(jnp.logical_not(even))
+    def _():
+        for c in range(NCH):
+            take_x(c)
+        for c in range(NCH):
+            conv_inner(c, c == 0)
+
+        @pl.when(has_up)
+        def _():
+            local_wait(lat_halo.at[0], lh_recv.at[0])
+
+        @pl.when(has_down)
+        def _():
+            local_wait(lat_halo.at[1], lh_recv.at[1])
+
+        for c in range(NCH):
+            take_edges(c)
+        for n in range(NCH):
+            conv_finish(n, range(NCH), False)
 
     def gather_copy(buf, kind, way):
         return remote(
@@ -494,7 +572,7 @@
 
     def g_copy(c):
         return pltpu.make_async_remote_copy(
-            src_ref=gs_img.at[:, lanes(c)], dst_ref=gin.at[:, lanes(c)],
+            src_ref=g_out.at[:, lanes(c)], dst_ref=gin.at[:, lanes(c)],
             send_sem=g_send.at[c], recv_sem=g_recv.at[c],
             device_id={"dp": dp, "section": s - 1}, device_id_type=MESH,
         )
@@ -520,6 +598,12 @@
         def _():
             local_wait(gin.at[:, lanes(c)], g_recv.at[c])
             gx[:, cols] = gin[:, cols].astype(F32)
+
+        for side, flag, rows in ((0, has_up, slice(0, COLS)), (1, has_down, slice(PIX - COLS, PIX))):
+            @pl.when(jnp.logical_and(flag, even))
+            def _():
+                local_wait(g_rim.at[side, :, lanes(c)], gr_recv.at[side, c])
+                gx[rows, cols] += g_rim[side, :, cols].astype(F32)
 
         grad_pre = (gx[:, cols] * dsilu[:, cols]).astype(BF16).astype(F32)
         gpv[0, :, cols] = after(grad_pre).astype(BF16)
@@ -537,36 +621,51 @@
             total = term if total is None else total + term
         return total
 
-    take_g(0)
-    for dr in (-1, 0, 1):
-        acc[dr + 1] = back_part(0, dr, every)
-    take_g(1)
-    for dr in (-1, 0, 1):
-        acc[dr + 1] += back_part(1, dr, every)
-    take_g(2)
-    for n in range(NCH):
+    def rim_direct_up(c):
+        return remote(
+            rim_out.at[0, :, lanes(c)], g_rim.at[1, :, lanes(c)], gr_send.at[0, c], gr_recv.at[1, c], up, s - 1
+        )
+
+    def rim_direct_down(c):
+        return remote(
+            rim_out.at[1, :, lanes(c)], g_rim.at[0, :, lanes(c)], gr_send.at[1, c], gr_recv.at[0, c], down, s - 1
+        )
+
+    def send_rims(n, upward, downward):
+        @pl.when(has_up)
+        def _():
+            upward(n).start()
+
+        @pl.when(has_down)
+        def _():
+            downward(n).start()
+
+    def back_rims(n, chunks, start):
         ncols = slice(n * CK, (n + 1) * CK)
-        upper = acc[0, :, ncols] + back_part(2, -1, ncols)
-        acc[0, :, ncols] = upper
-        rim_out[0, :, ncols] = upper[0:COLS].astype(BF16)
-        lower = acc[2, :, ncols] + back_part(2, 1, ncols)
-        acc[2, :, ncols] = lower
-        rim_out[1, :, ncols] = lower[PIX - COLS:].astype(BF16)
-
-        @pl.when(has_up)
-        def _():
-            rim_up(n).start()
-
-        @pl.when(has_down)
-        def _():
-            rim_down(n).start()
-
-    acc[1] += back_part(2, 0, every)
-    for n in range(NCH):
+        for side, dr in ((0, -1), (2, 1)):
+            total = None if start else acc[side, :, ncols]
+            for c in chunks:
+                term = back_part(c, dr, ncols)
+                total = term if total is None else total + term
+            acc[side, :, ncols] = total
+            if dr < 0:
+                rim_out[0, :, ncols] = total[0:COLS].astype(BF16)
+            else:
+                rim_out[1, :, ncols] = total[PIX - COLS:].astype(BF16)
+
+    def back_inner(n, chunks, start):
         ncols = slice(n * CK, (n + 1) * CK)
+        total = None if start else acc[1, :, ncols]
+        for c in chunks:
+            term = back_part(c, 0, ncols)
+            total = term if total is None else total + term
+        acc[1, :, ncols] = total
         acc[1, 0:PIX - COLS, ncols] += acc[0, COLS:, ncols]
         acc[1, COLS:, ncols] += acc[2, 0:PIX - COLS, ncols]
 
+    def add_rims(n):
+        ncols = slice(n * CK, (n + 1) * CK)
+
         @pl.when(has_up)
         def _():
             local_wait(rim_in.at[0, :, lanes(n)], rim_recv.at[0, n])
@@ -579,9 +678,52 @@
 
         gs_img[:, ncols] = acc[1, :, ncols].astype(BF16)
 
-        @pl.when(s > 0)
-        def _():
-            g_copy(n).start()
+    def send_g(n):
+        ncols = slice(n * CK, (n + 1) * CK)
+        g_out[:, ncols] = acc[1, :, ncols].astype(BF16)
+        g_copy(n).start()
+
+    @pl.when(jnp.logical_not(even))
+    def _():
+        take_g(0)
+        for dr in (-1, 0, 1):
+            acc[dr + 1] = back_part(0, dr, every)
+        take_g(1)
+        for dr in (-1, 0, 1):
+            acc[dr + 1] += back_part(1, dr, every)
+        take_g(2)
+        for n in range(NCH):
+            back_rims(n, (2,), False)
+            send_rims(n, rim_direct_up, rim_direct_down)
+            back_inner(n, (2,), False)
+            send_g(n)
+        for n in range(NCH):
+            send_rims(n, rim_up, rim_down)
+        for n in range(NCH):
+            add_rims(n)
+
+    @pl.when(even)
+    def _():
+        def finish(n):
+            back_inner(n, chunks, True)
+            add_rims(n)
+
+            @pl.when(s > 0)
+            def _():
+                send_g(n)
+
+        for c in range(NCH):
+            take_g(c)
+        chunks = range(NCH)
+        back_rims(0, chunks, True)
+        send_rims(0, rim_up, rim_down)
+        back_rims(1, chunks, True)
+        send_rims(1, rim_up, rim_down)
+        finish(0)
+        back_rims(2, chunks, True)
+        send_rims(2, rim_up, rim_down)
+        finish(1)
+        finish(2)
 
     def gz_copy(r):
         return remote(
@@ -624,7 +766,6 @@
     spread(x)
     spread(x_left)
     spread(x_right)
-    gather_forward(gs_all, 1)
     gather_finish(gp_all, 0)
     spread(x_far)
 
@@ -659,6 +800,7 @@
         ring_c[way, 0] = own_rows(part_c, CROWS, way, 0).astype(BF16)
         hop(*conv_ring, way, 0).start()
 
+    gather_forward(gs_all, 1)
     gather_finish(gs_all, 1)
     part_l[...] = nn(taps_t[...], gs_all[...].reshape(WIDE, CH))
 
@@ -719,13 +861,37 @@
 
         @pl.when(has_up)
         def _():
+            rim_up(c).wait_send()
+
+        @pl.when(has_down)
+        def _():
+            rim_down(c).wait_send()
+
+        @pl.when(jnp.logical_and(has_up, even))
+        def _():
             halo_up(c).wait_send()
-            rim_up(c).wait_send()
-
-        @pl.when(has_down)
+            edge_up(c).wait_send()
+
+        @pl.when(jnp.logical_and(has_down, even))
         def _():
             halo_down(c).wait_send()
-            rim_down(c).wait_send()
+            edge_down(c).wait_send()
+
+        @pl.when(jnp.logical_and(has_up, jnp.logical_not(even)))
+        def _():
+            rim_direct_up(c).wait_send()
+
+        @pl.when(jnp.logical_and(has_down, jnp.logical_not(even)))
+        def _():
+            rim_direct_down(c).wait_send()
+
+    @pl.when(jnp.logical_and(has_up, jnp.logical_not(even)))
+    def _():
+        lat_up().wait_send()
+
+    @pl.when(jnp.logical_and(has_down, jnp.logical_not(even)))
+    def _():
+        lat_down().wait_send()
 
     for kind, buf in enumerate((gp_all, gs_all, ext_all)):
         gather_sent(buf, kind)
@@ -774,6 +940,10 @@
             pltpu.VMEM((2, COLS, CH), BF16),
             pltpu.VMEM((2, 2 * COLS, CPAD), BF16),
             pltpu.VMEM((PIX, CPAD), BF16),
+            pltpu.VMEM((2, COLS, CH), BF16),
+            pltpu.VMEM((2, COLS, CH), BF16),
+            pltpu.VMEM((PIX, CH), BF16),
+            pltpu.VMEM((2, COLS, CH), BF16),
             pltpu.VMEM((NX, PIX + 2 * COLS, CH), BF16),
             pltpu.VMEM((NX, PIX, XL), BF16),
             pltpu.VMEM((PIX, CH), BF16),
@@ -809,6 +979,12 @@
             dma((NCH,)),
             dma((2, NCH)),
             dma((2, NCH)),
+            dma((2,)),
+            dma((2,)),
+            dma((2, NCH)),
+            dma((2, NCH)),
+            dma((2, NCH)),
+            dma((2, NCH)),
             pltpu.SemaphoreType.REGULAR,
             dma((4,)),
             dma((4,)),

time: 275 us -> 268 us (0.975)
  Pallas kernels: 267 us -> 260 us
    pallas_call x1, Pallas kernels: 267 us -> 260 us  [head_call(): pl.pallas_call(head_kernel, out_shape=(jax.ShapeDtypeStruct((CROWS, CH),...]
where the time goes in v5:
time: 268 us
  Pallas kernels  260 us (97%)
  local copies, waits for them, and re-layouts  7.45 us (3%)
    pallas_call x1, Pallas kernels, head_call(): pl.pallas_call(head_kernel, out_shape=(jax.ShapeDtypeStruct((CROWS, CH),...  260 us

profile of v5, /device:TPU:2, one launch (start us, length us, event | category | flops | bytes accessed | tf_op | source)
XLA Modules:
  0.0 267.8 jit_solution(10516060769504721141)
XLA Ops:
  0.6 1.6 pad.4.lat_ref
  2.2 1.9 copy.8.cls_ref
  4.1 259.8 %shard_map.77 = (f32[216,768]{1,0:T(8,128)}, f32[112,768]{1,0:T(8,128)}) custom-call(bf16[8,16,3200]{2,1,0:T(8,128)(2,1)} %bitcast.7, bf16[112,768]{1,0:T(8,128)(2,1)} %pad.4.lat_ref, bf16[9,768,768]{2,1,0:T(8,128)(2,1)} %bitcast.6, bf16[768,150]{1,0:T(8,128)(2,1)} %copy.8.cls_ref, s32[1,2]{1,0:T(1,128)} %counts_ref.1, s32[2,128]{1,0:T(2,128)} %labels_ref.1), custom_call_target="tpu_custom_call" | custom-call | tf_op jit(solution)/shard_map/pallas_call | solution.py:914
  263.8 1.0 slice_bitcast_fusion
  264.8 1.0 copy.9
  265.9 2.0 copy.11

commit v6 on v5

--- a/solution.py
+++ b/solution.py
@@ -44,8 +44,8 @@
 
 
 def head_kernel(
-    tap_ref, lat_ref, w_hbm, cls_ref, counts_ref, labels_ref, conv_out, lat_out,
-    tap_pad, wl, w, gx, lat_send, lat_far, lat_near, lat_nat, lat_img,
+    tap_ref, lat_ref, w_hbm, cls_hbm, counts_ref, labels_ref, conv_out, lat_out,
+    cls_ref, tap_pad, wl, w, gx, lat_send, lat_far, lat_near, lat_nat, lat_img,
     ext, xin, xout, gin, dsilu, acc, gpv, rim_out, rim_in, oh_own, oh,
     lat_halo, x_halo, g_out, g_rim,
     ext_all, taps_all, gs_img, gp_all, gs_all, gpv_all, cols_t, taps_t, part_c, part_l, ring_c, ring_l,
@@ -88,6 +88,11 @@
 
     w_copy = pltpu.make_async_copy(w_hbm, w, local_sem.at[0])
     w_copy.start()
+    cls_copy = pltpu.make_async_copy(cls_hbm, cls_ref, local_sem.at[1])
+
+    @pl.when(is_last)
+    def _():
+        cls_copy.start()
 
     barrier = pltpu.get_barrier_semaphore()
 
@@ -148,7 +153,9 @@
     def w_rows(zz):
         return wl.at[pl.ds(pl.multiple_of(zz * KPAD, 16), KPAD), :]
 
-    wl[pl.ds(pl.multiple_of(z * KPAD, 16), KPAD), :] = lat_ref[...]
+    wl[pl.ds(pl.multiple_of(z * KPAD, 16), KPAD), :] = jnp.concatenate(
+        [lat_ref[...].astype(F32), jnp.zeros((KPAD - KROWS, CH), F32)], 0
+    ).astype(BF16)
 
     need = jnp.where(even, 4 + 15, 4 + 16)
     for flag in (has_up, has_down, has_up, has_down, s > 0, s < SECTIONS - 1):
@@ -561,6 +568,7 @@
     def _():
         for r in range(4):
             local_wait(oh_rows(r), oh_recv.at[r])
+        cls_copy.wait()
         logits = nn(xout[...], cls_ref[...])
         spot = lax.broadcasted_iota(jnp.int32, (PIX, CPAD), 1)
         expo = jnp.exp(logits)
@@ -699,6 +707,7 @@
             send_g(n)
         for n in range(NCH):
             send_rims(n, rim_up, rim_down)
+        gather_start(gp_all, 0)
         for n in range(NCH):
             add_rims(n)
 
@@ -714,6 +723,11 @@
 
         for c in range(NCH):
             take_g(c)
+
+        @pl.when(is_first)
+        def _():
+            gather_start(gp_all, 0)
+
         chunks = range(NCH)
         back_rims(0, chunks, True)
         send_rims(0, rim_up, rim_down)
@@ -739,16 +753,15 @@
         def _():
             pltpu.make_async_copy(band(gs_img, r), band(gs_all.at[x], image), gz_recv.at[image]).start()
 
-    gather_start(gp_all, 0)
+    @pl.when(jnp.logical_and(even, s > 0))
+    def _():
+        gather_start(gp_all, 0)
 
     @pl.when(s >= 6)
     def _():
         early_start()
 
     gather_forward(gp_all, 0)
-    for img in range(4):
-        local_wait(band(gs_all.at[x], img), gz_recv.at[img])
-    gather_start(gs_all, 1)
 
     @pl.when(s >= 4)
     def _():
@@ -767,18 +780,25 @@
     spread(x_left)
     spread(x_right)
     gather_finish(gp_all, 0)
+    for img in range(4):
+        local_wait(band(gs_all.at[x], img), gz_recv.at[img])
+    gather_start(gs_all, 1)
     spread(x_far)
 
     @pl.when(s >= 4)
     def _():
         early_finish()
 
-    @pl.loop(0, 9)
-    def _(u):
+    def conv_unit(u):
         unit = 9 * x + u
         o = unit // 4
         chans = pl.ds(pl.multiple_of((unit % 4) * UNIT, UNIT), UNIT)
         part_c[pl.ds(pl.multiple_of(u * UNIT, UNIT), UNIT), :] = nn(cols_t[o // 3, chans, :], gpv_all[o % 3])
+
+    def conv_slice(zz):
+        @pl.loop(0, 2)
+        def _(k):
+            conv_unit(zz + k)
 
     def slice_at(way, t):
         return (z + NZ - 1 - t) % NZ if way == 0 else (z + 1 + t) % NZ
@@ -796,29 +816,59 @@
 
     conv_ring = (ring_c, rc_send, rc_recv)
     lat_ring = (ring_l, rl_send, rl_recv)
-    for way in range(2):
-        ring_c[way, 0] = own_rows(part_c, CROWS, way, 0).astype(BF16)
-        hop(*conv_ring, way, 0).start()
+    def ring_start(ring, part, rows):
+        for way in range(2):
+            ring[0][way, 0] = own_rows(part, rows, way, 0).astype(BF16)
+            hop(*ring, way, 0).start()
+
+    def ring_step(ring, part, rows, out, t):
+        buf = ring[0]
+        for way in range(2):
+            local_wait(buf.at[way, t + 1], ring[2].at[way, t])
+            total = buf[way, t + 1].astype(F32) + own_rows(part, rows, way, t + 1)
+            if t < NZ - 2:
+                buf[way, t + 1] = total.astype(BF16)
+                hop(*ring, way, t + 1).start()
+            else:
+                out[:, way * HALF:(way + 1) * HALF] = total
+
+    def conv_step(t):
+        ring_step(conv_ring, part_c, CROWS, conv_out, t)
+
+    def lat_step(t):
+        ring_step(lat_ring, part_l, KPAD, lat_out, t)
+
+    @pl.loop(0, 2)
+    def _(k):
+        conv_slice((z + 1 + k * (NZ - 2)) % NZ)
+
+    ring_start(conv_ring, part_c, CROWS)
+
+    @pl.loop(0, 2)
+    def _(k):
+        conv_slice((z + 2 + k * (NZ - 4)) % NZ)
 
     gather_forward(gs_all, 1)
+    conv_step(0)
+
+    @pl.loop(0, 2)
+    def _(k):
+        conv_slice((z + 3 + k * (NZ - 6)) % NZ)
+
     gather_finish(gs_all, 1)
     part_l[...] = nn(taps_t[...], gs_all[...].reshape(WIDE, CH))
-
-    for way in range(2):
-        ring_l[way, 0] = own_rows(part_l, KPAD, way, 0).astype(BF16)
-        hop(*lat_ring, way, 0).start()
-
-    for t in range(NZ - 1):
-        for ring, part, rows, out in ((conv_ring, part_c, CROWS, conv_out), (lat_ring, part_l, KPAD, lat_out)):
-            for way in range(2):
-                buf = ring[0]
-                local_wait(buf.at[way, t + 1], ring[2].at[way, t])
-                total = buf[way, t + 1].astype(F32) + own_rows(part, rows, way, t + 1)
-                if t < NZ - 2:
-                    buf[way, t + 1] = total.astype(BF16)
-                    hop(*ring, way, t + 1).start()
-                else:
-                    out[:, way * HALF:(way + 1) * HALF] = total
+    ring_start(lat_ring, part_l, KPAD)
+    conv_step(1)
+
+    @pl.loop(0, 2)
+    def _(k):
+        conv_slice((z + 4 * k) % NZ)
+
+    lat_step(0)
+    for t in range(2, NZ - 1):
+        conv_step(t)
+        lat_step(t - 1)
+    lat_step(NZ - 2)
 
     for k in range(8):
         for xx in range(NX):
@@ -917,9 +967,10 @@
             jax.ShapeDtypeStruct((CROWS, CH), F32),
             jax.ShapeDtypeStruct((KPAD, CH), F32),
         ),
-        in_specs=[vmem, vmem, hbm, vmem, smem, vmem],
+        in_specs=[vmem, vmem, hbm, hbm, smem, vmem],
         out_specs=(vmem, vmem),
         scratch_shapes=[
+            pltpu.VMEM((CH, CLASSES), BF16),
             pltpu.VMEM((8, 16, KW), BF16),
             pltpu.VMEM((XL, CH), BF16),
             pltpu.VMEM((9, CH, CH), BF16),
@@ -956,7 +1007,7 @@
             pltpu.VMEM((XL, CH), F32),
             pltpu.VMEM((2, NZ, CROWS, HALF), BF16),
             pltpu.VMEM((2, NZ, KPAD, HALF), BF16),
-            dma((1,)),
+            dma((2,)),
             dma((8, NX)),
             dma((NX, 2 * SECTIONS)),
             dma((NX,)),
@@ -1004,9 +1055,8 @@
 def on_device(tap_maps, lateral_weight, conv_weight, classifier, tile_counts, labels):
     levels, micros, here, width = tap_maps.shape
     taps = tap_maps.reshape(levels * micros, here, width)
-    lat = jnp.pad(lateral_weight[0], ((0, KPAD - KROWS), (0, 0)))
     conv_grad, lateral_grad = head_call(
-        taps, lat, conv_weight.reshape(9, CH, CH), classifier, tile_counts, labels
+        taps, lateral_weight[0], conv_weight.reshape(9, CH, CH), classifier, tile_counts, labels
     )
     return (conv_grad[None], lateral_grad[None, :KROWS])
 

time: 268 us -> 266 us (level)
  no operation moved by 1% of the time
where the time goes in v6:
time: 266 us; the launch traced here: 265 us
  Pallas kernels  259 us (97%)
  local copies, waits for them, and re-layouts  5.86 us (2%)
    pallas_call x1, Pallas kernels, head_call(): pl.pallas_call(head_kernel, out_shape=(jax.ShapeDtypeStruct((CROWS, CH),...  259 us

profile of v6, /device:TPU:2, one launch (start us, length us, event | category | flops | bytes accessed | tf_op | source)
XLA Modules:
  0.0 265.2 jit_solution(18135621739876935404)
XLA Ops:
  0.6 1.9 copy.8.cls_hbm
  2.5 258.7 %shard_map.77 = (f32[216,768]{1,0:T(8,128)}, f32[112,768]{1,0:T(8,128)}) custom-call(bf16[8,16,3200]{2,1,0:T(8,128)(2,1)} %bitcast.7, bf16[100,768]{1,0:T(8,128)(2,1)} %bitcast.9, bf16[9,768,768]{2,1,0:T(8,128)(2,1)} %bitcast.6, bf16[768,150]{1,0:T(8,128)(2,1)} %copy.8.cls_hbm, s32[1,2]{1,0:T(1,128)} %counts_ref.1, s32[2,128]{1,0:T(2,128)} %labels_ref.1), custom_call_target="tpu_custom_call" | custom-call | tf_op jit(solution)/shard_map/pallas_call | solution.py:964
  261.2 1.0 slice_bitcast_fusion
  262.2 1.0 copy.9
  263.3 2.0 copy.11

commit v7 on v6

--- a/solution.py
+++ b/solution.py
@@ -49,7 +49,7 @@
     ext, xin, xout, gin, dsilu, acc, gpv, rim_out, rim_in, oh_own, oh,
     lat_halo, x_halo, g_out, g_rim,
     ext_all, taps_all, gs_img, gp_all, gs_all, gpv_all, cols_t, taps_t, part_c, part_l, ring_c, ring_l,
-    local_sem, tap_send, tap_recv, pass_send, pass_recv, wz_send, w_recv,
+    gate_sem, local_sem, tap_send, tap_recv, pass_send, pass_recv, wz_send, w_recv,
     lf_send, lf_recv, ln_send, ln_recv, lz_send, lz_recv, oh_send, oh_recv,
     x_send, x_recv, halo_send, halo_recv, g_send, g_recv, rim_send, rim_recv,
     lh_send, lh_recv, xh_send, xh_recv, gr_send, gr_recv,
@@ -182,17 +182,6 @@
     def elsewhere(k, xx):
         return jnp.logical_or(xx != x, k // 2 * 2 != s)
 
-    for k in range(8):
-        for xx in range(NX):
-            @pl.when(elsewhere(k, xx))
-            def _():
-                tap_copy(k, xx).start()
-
-            @pl.when(jnp.logical_not(elsewhere(k, xx)))
-            def _():
-                slot = (k % 2) * SECTIONS + s
-                pltpu.make_async_copy(tap_src(k, xx), tap_cell(x, slot), tap_recv.at[x, slot]).start()
-
     order = (0, -1, 1, -2, 2, -3, 3, -4)
 
     def ring_z(i):
@@ -210,11 +199,41 @@
             ways.append(1)
         return ways
 
-    for i in range(NZ):
+    def w_step(i):
         if i > 0:
             local_wait(w_rows(ring_z(i)), w_recv.at[ring_z(i)])
         for way in z_ways(i):
             w_send_z(i, way).start()
+
+    @pl.when(even)
+    def _():
+        w_step(0)
+
+    for k in range(8):
+        for xx in range(NX):
+            @pl.when(elsewhere(k, xx))
+            def _():
+                tap_copy(k, xx).start()
+
+            @pl.when(jnp.logical_not(elsewhere(k, xx)))
+            def _():
+                slot = (k % 2) * SECTIONS + s
+                pltpu.make_async_copy(tap_src(k, xx), tap_cell(x, slot), tap_recv.at[x, slot]).start()
+
+    def pass_turn(k):
+        pl.semaphore_signal(gate_sem.at[k], inc=1, device_id={"dp": dp, "section": s + 1}, device_id_type=MESH)
+
+    @pl.when(even)
+    def _():
+        for i in range(1, NZ):
+            w_step(i)
+        pass_turn(0)
+
+    @pl.when(jnp.logical_not(even))
+    def _():
+        pl.semaphore_wait(gate_sem.at[0], 1)
+        for i in range(NZ):
+            w_step(i)
 
     def oh_rows(r):
         return oh.at[pl.ds(pl.multiple_of(r * COLS, COLS), COLS), :]
@@ -280,6 +299,11 @@
         )
 
     lat_send[2] = nn(taps_all[x_far], wl[...]).astype(BF16)
+
+    @pl.when(jnp.logical_not(even))
+    def _():
+        pl.semaphore_wait(gate_sem.at[1], 1)
+
     for way in range(2):
         far_copy(way).start()
     for way in range(2):
@@ -301,6 +325,10 @@
             acc[2, rows] + lat_near[0, rows].astype(F32) + lat_near[1, rows].astype(F32)
         ).astype(BF16)
 
+    @pl.when(even)
+    def _():
+        pass_turn(1)
+
     def band(ref, j):
         return ref.at[pl.ds(pl.multiple_of(j * COLS, COLS), COLS), :]
 
@@ -569,14 +597,14 @@
         for r in range(4):
             local_wait(oh_rows(r), oh_recv.at[r])
         cls_copy.wait()
-        logits = nn(xout[...], cls_ref[...])
+        logits = nt(xout[...], cls_ref[...])
         spot = lax.broadcasted_iota(jnp.int32, (PIX, CPAD), 1)
         expo = jnp.exp(logits)
         probs = expo / jnp.sum(expo, axis=-1, keepdims=True)
         marks = oh[...].astype(F32)
         weight = jnp.sum(jnp.where(spot == CPAD - 1, marks, 0.0), axis=-1, keepdims=True)
         grad_logits = ((probs - marks[:, :CLASSES]) * weight).astype(BF16)
-        gx[...] = nt(grad_logits, cls_ref[...])
+        gx[...] = nn(grad_logits, cls_ref[...])
 
     def g_copy(c):
         return pltpu.make_async_remote_copy(
@@ -970,7 +998,7 @@
         in_specs=[vmem, vmem, hbm, hbm, smem, vmem],
         out_specs=(vmem, vmem),
         scratch_shapes=[
-            pltpu.VMEM((CH, CLASSES), BF16),
+            pltpu.VMEM((CLASSES, CH), BF16),
             pltpu.VMEM((8, 16, KW), BF16),
             pltpu.VMEM((XL, CH), BF16),
             pltpu.VMEM((9, CH, CH), BF16),
@@ -1007,6 +1035,7 @@
             pltpu.VMEM((XL, CH), F32),
             pltpu.VMEM((2, NZ, CROWS, HALF), BF16),
             pltpu.VMEM((2, NZ, KPAD, HALF), BF16),
+            pltpu.SemaphoreType.REGULAR((2,)),
             dma((2,)),
             dma((8, NX)),
             dma((NX, 2 * SECTIONS)),
@@ -1056,7 +1085,7 @@
     levels, micros, here, width = tap_maps.shape
     taps = tap_maps.reshape(levels * micros, here, width)
     conv_grad, lateral_grad = head_call(
-        taps, lateral_weight[0], conv_weight.reshape(9, CH, CH), classifier, tile_counts, labels
+        taps, lateral_weight[0], conv_weight.reshape(9, CH, CH), classifier.T, tile_counts, labels
     )
     return (conv_grad[None], lateral_grad[None, :KROWS])
 

time: 266 us -> 261 us (0.981)
  Pallas kernels: 259 us -> 256 us
where the time goes in v7:
time: 261 us
  Pallas kernels  256 us (98%)
  local copies, waits for them, and re-layouts  4 us (2%)
    pallas_call x1, Pallas kernels, head_call(): pl.pallas_call(head_kernel, out_shape=(jax.ShapeDtypeStruct((CROWS, CH),...  256 us

profile of v7, /device:TPU:2, one launch (start us, length us, event | category | flops | bytes accessed | tf_op | source)
XLA Modules:
  0.0 260.9 jit_solution(18007824439998562192)
XLA Ops:
  0.6 256.3 %shard_map.77 = (f32[216,768]{1,0:T(8,128)}, f32[112,768]{1,0:T(8,128)}) custom-call(bf16[8,16,3200]{2,1,0:T(8,128)(2,1)} %bitcast.8, bf16[100,768]{1,0:T(8,128)(2,1)} %bitcast.11, bf16[9,768,768]{2,1,0:T(8,128)(2,1)} %bitcast.7, bf16[150,768]{1,0:T(8,128)(2,1)} %bitcast.10, s32[1,2]{1,0:T(1,128)} %counts_ref.1, s32[2,128]{1,0:T(2,128)} %labels_ref.1), custom_call_target="tpu_custom_call" | custom-call | tf_op jit(solution)/shard_map/pallas_call | solution.py:992
  256.9 1.0 slice_bitcast_fusion
  257.9 1.0 copy.8
  259.0 2.0 copy.10

commit v8 on v7

--- a/solution.py
+++ b/solution.py
@@ -209,28 +209,37 @@
     def _():
         w_step(0)
 
-    for k in range(8):
-        for xx in range(NX):
-            @pl.when(elsewhere(k, xx))
-            def _():
-                tap_copy(k, xx).start()
-
-            @pl.when(jnp.logical_not(elsewhere(k, xx)))
-            def _():
-                slot = (k % 2) * SECTIONS + s
-                pltpu.make_async_copy(tap_src(k, xx), tap_cell(x, slot), tap_recv.at[x, slot]).start()
+    def send_taps(ks):
+        for k in ks:
+            for xx in range(NX):
+                @pl.when(elsewhere(k, xx))
+                def _():
+                    tap_copy(k, xx).start()
+
+                @pl.when(jnp.logical_not(elsewhere(k, xx)))
+                def _():
+                    slot = (k % 2) * SECTIONS + s
+                    pltpu.make_async_copy(tap_src(k, xx), tap_cell(x, slot), tap_recv.at[x, slot]).start()
+
+    send_taps(range(2))
 
     def pass_turn(k):
         pl.semaphore_signal(gate_sem.at[k], inc=1, device_id={"dp": dp, "section": s + 1}, device_id_type=MESH)
 
     @pl.when(even)
     def _():
-        for i in range(1, NZ):
+        for i in range(1, NZ // 2 + 1):
+            w_step(i)
+        pass_turn(2)
+        send_taps(range(2, 8))
+        for i in range(NZ // 2 + 1, NZ):
             w_step(i)
         pass_turn(0)
 
     @pl.when(jnp.logical_not(even))
     def _():
+        pl.semaphore_wait(gate_sem.at[2], 1)
+        send_taps(range(2, 8))
         pl.semaphore_wait(gate_sem.at[0], 1)
         for i in range(NZ):
             w_step(i)
@@ -735,9 +744,18 @@
             send_g(n)
         for n in range(NCH):
             send_rims(n, rim_up, rim_down)
-        gather_start(gp_all, 0)
+
+        @pl.when(s == 1)
+        def _():
+            gather_start(gp_all, 0)
+
         for n in range(NCH):
             add_rims(n)
+
+        @pl.when(s > 1)
+        def _():
+            pl.semaphore_wait(gate_sem.at[3], 1)
+            gather_start(gp_all, 0)
 
     @pl.when(even)
     def _():
@@ -766,6 +784,10 @@
         send_rims(2, rim_up, rim_down)
         finish(1)
         finish(2)
+
+        @pl.when(s > 0)
+        def _():
+            pass_turn(3)
 
     def gz_copy(r):
         return remote(
@@ -1035,7 +1057,7 @@
             pltpu.VMEM((XL, CH), F32),
             pltpu.VMEM((2, NZ, CROWS, HALF), BF16),
             pltpu.VMEM((2, NZ, KPAD, HALF), BF16),
-            pltpu.SemaphoreType.REGULAR((2,)),
+            pltpu.SemaphoreType.REGULAR((4,)),
             dma((2,)),
             dma((8, NX)),
             dma((NX, 2 * SECTIONS)),

time: 261 us -> 256 us (0.981)
  Pallas kernels: 256 us -> 251 us
    pallas_call x1, Pallas kernels: 256 us -> 251 us  [head_call(): pl.pallas_call(head_kernel, out_shape=(jax.ShapeDtypeStruct((CROWS, CH),...]
where the time goes in v8:
time: 256 us
  Pallas kernels  251 us (98%)
  local copies, waits for them, and re-layouts  4 us (2%)
    pallas_call x1, Pallas kernels, head_call(): pl.pallas_call(head_kernel, out_shape=(jax.ShapeDtypeStruct((CROWS, CH),...  251 us

profile of v8, /device:TPU:2, one launch (start us, length us, event | category | flops | bytes accessed | tf_op | source)
XLA Modules:
  0.0 256.0 jit_solution(13613795805685008410)
XLA Ops:
  0.6 251.4 %shard_map.77 = (f32[216,768]{1,0:T(8,128)}, f32[112,768]{1,0:T(8,128)}) custom-call(bf16[8,16,3200]{2,1,0:T(8,128)(2,1)} %bitcast.8, bf16[100,768]{1,0:T(8,128)(2,1)} %bitcast.11, bf16[9,768,768]{2,1,0:T(8,128)(2,1)} %bitcast.7, bf16[150,768]{1,0:T(8,128)(2,1)} %bitcast.10, s32[1,2]{1,0:T(1,128)} %counts_ref.1, s32[2,128]{1,0:T(2,128)} %labels_ref.1), custom_call_target="tpu_custom_call" | custom-call | tf_op jit(solution)/shard_map/pallas_call | solution.py:1014
  252.0 1.0 slice_bitcast_fusion
  253.0 1.0 copy.8
  254.1 2.0 copy.10

commit v9 on v8

--- a/solution.py
+++ b/solution.py
@@ -137,18 +137,22 @@
             def _():
                 greet(d, s)
 
-    flat = tap_ref[...].reshape(8 * 16, GROUPS * KROWS).astype(F32)
-    lane = lax.broadcasted_iota(jnp.int32, (8 * 16, 128), 1)
-    for tile in range(KW // 128):
-        first = tile * 128
-        total = jnp.zeros((8 * 16, 128), F32)
-        for g in range(first // KPAD, min((first + 127) // KPAD + 1, GROUPS)):
-            lo = first - (KPAD - KROWS) * g
-            start = min(max(lo // 128 * 128, 0), GROUPS * KROWS - 256)
-            moved = pltpu.roll(flat[:, start:start + 256], (start - lo) % 256, 1)[:, :128]
-            inside = jnp.logical_and(lane + first >= KPAD * g, lane + first < KPAD * g + KROWS)
-            total = jnp.where(inside, moved, total)
-        tap_pad[:, :, first:first + 128] = total.astype(BF16).reshape(8, 16, 128)
+    def pad_taps(k0, k1):
+        rows = (k1 - k0) * 16
+        flat = tap_ref[k0:k1].reshape(rows, GROUPS * KROWS).astype(F32)
+        lane = lax.broadcasted_iota(jnp.int32, (rows, 128), 1)
+        for tile in range(KW // 128):
+            first = tile * 128
+            total = jnp.zeros((rows, 128), F32)
+            for g in range(first // KPAD, min((first + 127) // KPAD + 1, GROUPS)):
+                lo = first - (KPAD - KROWS) * g
+                start = min(max(lo // 128 * 128, 0), GROUPS * KROWS - 256)
+                moved = pltpu.roll(flat[:, start:start + 256], (start - lo) % 256, 1)[:, :128]
+                inside = jnp.logical_and(lane + first >= KPAD * g, lane + first < KPAD * g + KROWS)
+                total = jnp.where(inside, moved, total)
+            tap_pad[k0:k1, :, first:first + 128] = total.astype(BF16).reshape(k1 - k0, 16, 128)
+
+    pad_taps(0, 2)
 
     def w_rows(zz):
         return wl.at[pl.ds(pl.multiple_of(zz * KPAD, 16), KPAD), :]
@@ -222,6 +226,7 @@
                     pltpu.make_async_copy(tap_src(k, xx), tap_cell(x, slot), tap_recv.at[x, slot]).start()
 
     send_taps(range(2))
+    pad_taps(2, 8)
 
     def pass_turn(k):
         pl.semaphore_signal(gate_sem.at[k], inc=1, device_id={"dp": dp, "section": s + 1}, device_id_type=MESH)
@@ -880,7 +885,7 @@
                 buf[way, t + 1] = total.astype(BF16)
                 hop(*ring, way, t + 1).start()
             else:
-                out[:, way * HALF:(way + 1) * HALF] = total
+                out[:, way * HALF:(way + 1) * HALF] = total[0:out.shape[0]]
 
     def conv_step(t):
         ring_step(conv_ring, part_c, CROWS, conv_out, t)
@@ -1015,7 +1020,7 @@
         head_kernel,
         out_shape=(
             jax.ShapeDtypeStruct((CROWS, CH), F32),
-            jax.ShapeDtypeStruct((KPAD, CH), F32),
+            jax.ShapeDtypeStruct((KROWS, CH), F32),
         ),
         in_specs=[vmem, vmem, hbm, hbm, smem, vmem],
         out_specs=(vmem, vmem),
@@ -1109,7 +1114,7 @@
     conv_grad, lateral_grad = head_call(
         taps, lateral_weight[0], conv_weight.reshape(9, CH, CH), classifier.T, tile_counts, labels
     )
-    return (conv_grad[None], lateral_grad[None, :KROWS])
+    return (conv_grad[None], lateral_grad[None])
 
 
 def solution(mesh):

time: 256 us -> 256 us (level)
  no operation moved by 1% of the time
where the time goes in v9:
time: 256 us
  Pallas kernels  251 us (98%)
  local copies, waits for them, and re-layouts  3.97 us (2%)
    pallas_call x1, Pallas kernels, head_call(): pl.pallas_call(head_kernel, out_shape=(jax.ShapeDtypeStruct((CROWS, CH),...  251 us

profile of v9, /device:TPU:2, one launch (start us, length us, event | category | flops | bytes accessed | tf_op | source)
XLA Modules:
  0.0 256.0 jit_solution(11840899518162392656)
XLA Ops:
  0.6 251.4 %shard_map.77 = (f32[216,768]{1,0:T(8,128)}, f32[100,768]{1,0:T(8,128)}) custom-call(bf16[8,16,3200]{2,1,0:T(8,128)(2,1)} %bitcast.7, bf16[100,768]{1,0:T(8,128)(2,1)} %bitcast.11, bf16[9,768,768]{2,1,0:T(8,128)(2,1)} %bitcast.6, bf16[150,768]{1,0:T(8,128)(2,1)} %bitcast.10, s32[1,2]{1,0:T(1,128)} %counts_ref.1, s32[2,128]{1,0:T(2,128)} %labels_ref.1), custom_call_target="tpu_custom_call" | custom-call | tf_op jit(solution)/shard_map/pallas_call | solution.py:1019
  252.0 2.0 copy.8
  254.0 2.0 copy.10
